TPU v7x, 256 devices: a whole 4x4x8 slice. The times are simulated.
256 devices in a mesh: energy: 32 (over x_lo, z, core), mom: 8 (over x_hi, y).
Axes of the slice: x: 4 (x_hi: 2, x_lo: 2; x = x_hi * 2 + x_lo), y: 4, z: 8, core: 2. Of those that a mesh axis runs over, the one named last changes fastest.
Arguments:
- sigma_in: float32 [128, 8, 2, 256, 256], P('energy', 'mom'), may hold values from -0.1875 to 0.1875
- hamiltonian: float32 [8, 2, 256, 256], P('mom'), may hold values from -0.375 to 0.375
- coupling: float32 [8, 256, 256], P('mom'), may hold values from -0.1875 to 0.1875
- energies: float32 [128], replicated, may hold values from 1.4 to 2, as said below
- counts: int32 [128], replicated, may hold values from 2 to 4, as said below
- strengths: float32 [16], replicated, may hold values from 0.05625 to 0.1875
- offsets: int32 [16], replicated, may hold values from 0 to 7
Outputs:
- sigma_next: float32 [128, 8, 2, 256, 256], P('energy', 'mom')
Inputs may be any that keep to these rules, and one draw needn't show every extreme that they name: `energies`: increasing along the grid. `counts`: each point needs either 2 or 4 sweeps, and some point needs 4.
All inputs are finite; a program needn't handle non-finite values.
Results may differ from a plain program's by a relative error of at most 0.0003.
Values sent between devices are 32-bit elements; how exact they have to be, the bound alone decides.
No kernel may reach another device: no remote copies, remote signals or barrier semaphores. Data moves between devices by JAX's collectives and lax.ppermute only.
A program may use at most 64 MiB of HBM per device.

v0:
```python
import jax
import jax.numpy as jnp
from jax import lax
from jax.sharding import PartitionSpec as P

PRECISE = lax.Precision.HIGHEST
MIX_RATE = 0.6
PHONON = 0.1
BROADENING = 0.02


def product(left_side, right_side):
    return jnp.dot(left_side, right_side, precision=PRECISE, preferred_element_type=jnp.float32)


def invert(matrix, energy, sweeps):
    identity = jnp.eye(matrix.shape[0], dtype=jnp.float32)

    def keep_going(carried):
        return carried[0] < sweeps

    def sweep(carried):
        estimate = carried[1]
        return (carried[0] + 1, 2.0 * estimate - product(estimate, product(matrix, estimate)))

    return lax.while_loop(keep_going, sweep, (jnp.int32(0), identity / energy))[1]


def solve_point(ham_block, coupling_block, sigma_pair, energy, sweeps):
    identity = jnp.eye(ham_block.shape[1], dtype=jnp.float32)
    left_matrix = energy * identity - ham_block[0] - sigma_pair[0]
    left_inverse = invert(left_matrix, energy, sweeps)
    inverse_coupled = product(left_inverse, coupling_block)
    coupled_inverse = product(coupling_block.T, left_inverse)
    right_matrix = (
        energy * identity
        - ham_block[1]
        - sigma_pair[1]
        - product(coupling_block.T, inverse_coupled)
    )
    right_green = invert(right_matrix, energy, sweeps)
    left_green = left_inverse + product(product(inverse_coupled, right_green), coupled_inverse)
    return jnp.stack([left_green, right_green])


def lorentz(offset):
    scaled = offset / BROADENING
    return 1.0 / (1.0 + scaled * scaled)


def build_kernel(row_energy, column_energy):
    spacing = row_energy[:, None] - column_energy[None, :]
    kernel = lorentz(spacing - PHONON) + lorentz(spacing + PHONON)
    return kernel / jnp.sum(kernel, axis=1, keepdims=True)


def body(sigma_in, hamiltonian, coupling, energies, counts, strengths, offsets):
    points = sigma_in.shape[0]
    order = sigma_in.shape[3]
    ranks = lax.axis_size("energy")
    moments = lax.axis_size("mom")
    my_rank = lax.axis_index("energy")
    own_energy = lax.dynamic_slice_in_dim(energies, my_rank * points, points)
    own_count = lax.dynamic_slice_in_dim(counts, my_rank * points, points)
    blocks = sigma_in[:, 0]

    def solve_held(held_point):
        return solve_point(hamiltonian[0], coupling[0], held_point[0], held_point[1], held_point[2])

    green_blocks = lax.map(solve_held, (blocks, own_energy, own_count))
    shift_index = jnp.arange(moments, dtype=jnp.int32)
    weights = jnp.sum(
        strengths[:, None] * (offsets[:, None] == shift_index[None, :]).astype(jnp.float32), axis=0
    )
    kernel = build_kernel(energies, energies)
    piece_width = 2 * order * order // ranks
    spread = green_blocks.reshape(points, ranks, moments, piece_width // moments)
    column = lax.all_to_all(spread, "energy", split_axis=1, concat_axis=0, tiled=True)[:, 0]
    momentum_rows = lax.all_to_all(column, "mom", split_axis=1, concat_axis=1, tiled=True)
    mixed_rows = weights[0] * momentum_rows
    for offset_step in range(1, moments):
        mixed_rows = mixed_rows + weights[offset_step] * jnp.roll(
            momentum_rows, offset_step, axis=1
        )
    folded = jnp.einsum("ae,ekn->akn", kernel, mixed_rows, precision=PRECISE)
    sigma_part = lax.all_to_all(folded, "mom", split_axis=1, concat_axis=1, tiled=True)
    result = lax.all_to_all(sigma_part[:, None], "energy", split_axis=0, concat_axis=1, tiled=True)
    sigma_new = result.reshape(sigma_in.shape)
    return (1.0 - MIX_RATE) * sigma_in + MIX_RATE * sigma_new


def solution(mesh):
    placed = (
        P("energy", "mom", None, None, None),
        P("mom", None, None, None),
        P("mom", None, None),
        P(),
        P(),
        P(),
        P(),
    )
    return jax.shard_map(
        body,
        mesh=mesh,
        in_specs=placed,
        out_specs=P("energy", "mom", None, None, None),
        check_vma=False,
    )
```

profile of v0, /device:TPU:1, one launch (start us, length us, event | category | flops | bytes accessed | tf_op | source)
XLA Modules:
  0.0 296.2 jit_solution(4401892094808195605)
XLA Ops:
  0.0 0.7 dynamic_slice.19
  0.7 0.7 dynamic_slice.18
  1.5 1.2 copy.40
  2.7 3.0 copy.39
  5.7 72.0 %while.32 = (s32[]{:T(128)}, f32[4,2,256,256]{3,2,1,0:T(8,128)}, f32[4]{0:T(128)S(1)}, s32[4]{0:T(128)S(1)}, f32[1,2,256,256]{2,3,1,0:T(8,128)S(1)}, /*index=5*/...) while((s32[]{:T(128)}, f32[4,2,256,256]{3,2,1,0:T(8,128)}, ...), condition=%wide.region_7.8_spmd, body=%wide.region_2.7_spmd.sunk | while | flops 1813118976 | bytes 13631915 | solution.py:70
  5.7 0.6 dynamic_slice.22
  7.5 1.6 fusion.131
  9.3 7.0 %while.33 = (s32[]{:T(128)}, f32[256,256]{0,1:T(8,128)S(1)}, s32[]{:T(128)}, f32[256,256]{1,0:T(8,128)S(1)}, s32[]{:T(128)}) while((s32[]{:T(128)}, f32[256,256]{0,1:T(8,128)S(1)}, s32[]{:T(128)}, f32[256,256]{1,0:T(8,128)S(1)}, s32[]{:T(128)}) %tuple.76), condition=%wide.region_4.4_spmd, body=%wide.region_3.3_spmd.sunk | while | flops 402784256 | bytes 2097213 | solution.py:26
  10.3 0.6 fusion.143
  11.9 0.6 fusion.143
  13.5 0.6 fusion.143
  15.1 0.6 fusion.143
  16.3 0.6 fusion.132
  16.9 2.2 fusion.133
  19.2 7.0 %while.34 = (s32[]{:T(128)}, f32[256,256]{0,1:T(8,128)S(1)}, s32[]{:T(128)}, f32[256,256]{1,0:T(8,128)S(1)}, s32[]{:T(128)}) while((s32[]{:T(128)}, f32[256,256]{0,1:T(8,128)S(1)}, s32[]{:T(128)}, f32[256,256]{1,0:T(8,128)S(1)}, s32[]{:T(128)}) %tuple.79), condition=%wide.region_6.6_spmd, body=%wide.region_5.5_spmd.sunk | while | flops 402784256 | bytes 2097213 | solution.py:26
  20.2 0.6 fusion.149
  21.8 0.6 fusion.149
  23.4 0.6 fusion.149
  25.0 0.6 fusion.149
  27.7 0.8 fusion.137
  28.5 0.6 dynamic_slice.22
  30.4 1.6 fusion.131
  32.1 3.8 %while.33 = (s32[]{:T(128)}, f32[256,256]{0,1:T(8,128)S(1)}, s32[]{:T(128)}, f32[256,256]{1,0:T(8,128)S(1)}, s32[]{:T(128)}) while((s32[]{:T(128)}, f32[256,256]{0,1:T(8,128)S(1)}, s32[]{:T(128)}, f32[256,256]{1,0:T(8,128)S(1)}, s32[]{:T(128)}) %tuple.76), condition=%wide.region_4.4_spmd, body=%wide.region_3.3_spmd.sunk | while | flops 402784256 | bytes 2097213 | solution.py:26
  33.1 0.6 fusion.143
  34.7 0.6 fusion.143
  36.5 2.2 fusion.133
  38.8 3.8 %while.34 = (s32[]{:T(128)}, f32[256,256]{0,1:T(8,128)S(1)}, s32[]{:T(128)}, f32[256,256]{1,0:T(8,128)S(1)}, s32[]{:T(128)}) while((s32[]{:T(128)}, f32[256,256]{0,1:T(8,128)S(1)}, s32[]{:T(128)}, f32[256,256]{1,0:T(8,128)S(1)}, s32[]{:T(128)}) %tuple.79), condition=%wide.region_6.6_spmd, body=%wide.region_5.5_spmd.sunk | while | flops 402784256 | bytes 2097213 | solution.py:26
  39.8 0.6 fusion.149
  41.4 0.6 fusion.149
  44.1 0.8 fusion.137
  44.9 0.6 dynamic_slice.22
  46.8 1.6 fusion.131
  48.5 3.8 %while.33 = (s32[]{:T(128)}, f32[256,256]{0,1:T(8,128)S(1)}, s32[]{:T(128)}, f32[256,256]{1,0:T(8,128)S(1)}, s32[]{:T(128)}) while((s32[]{:T(128)}, f32[256,256]{0,1:T(8,128)S(1)}, s32[]{:T(128)}, f32[256,256]{1,0:T(8,128)S(1)}, s32[]{:T(128)}) %tuple.76), condition=%wide.region_4.4_spmd, body=%wide.region_3.3_spmd.sunk | while | flops 402784256 | bytes 2097213 | solution.py:26
  49.5 0.6 fusion.143
  51.1 0.6 fusion.143
  52.3 0.6 fusion.132
  52.9 2.2 fusion.133
  55.2 3.8 %while.34 = (s32[]{:T(128)}, f32[256,256]{0,1:T(8,128)S(1)}, s32[]{:T(128)}, f32[256,256]{1,0:T(8,128)S(1)}, s32[]{:T(128)}) while((s32[]{:T(128)}, f32[256,256]{0,1:T(8,128)S(1)}, s32[]{:T(128)}, f32[256,256]{1,0:T(8,128)S(1)}, s32[]{:T(128)}) %tuple.79), condition=%wide.region_6.6_spmd, body=%wide.region_5.5_spmd.sunk | while | flops 402784256 | bytes 2097213 | solution.py:26
  56.2 0.6 fusion.149
  57.8 0.6 fusion.149
  60.5 0.8 fusion.137
  61.3 0.6 dynamic_slice.22
  63.2 1.6 fusion.131
  64.9 3.8 %while.33 = (s32[]{:T(128)}, f32[256,256]{0,1:T(8,128)S(1)}, s32[]{:T(128)}, f32[256,256]{1,0:T(8,128)S(1)}, s32[]{:T(128)}) while((s32[]{:T(128)}, f32[256,256]{0,1:T(8,128)S(1)}, s32[]{:T(128)}, f32[256,256]{1,0:T(8,128)S(1)}, s32[]{:T(128)}) %tuple.76), condition=%wide.region_4.4_spmd, body=%wide.region_3.3_spmd.sunk | while | flops 402784256 | bytes 2097213 | solution.py:26
  65.9 0.6 fusion.143
  67.5 0.6 fusion.143
  69.3 2.2 fusion.133
  71.6 3.8 %while.34 = (s32[]{:T(128)}, f32[256,256]{0,1:T(8,128)S(1)}, s32[]{:T(128)}, f32[256,256]{1,0:T(8,128)S(1)}, s32[]{:T(128)}) while((s32[]{:T(128)}, f32[256,256]{0,1:T(8,128)S(1)}, s32[]{:T(128)}, f32[256,256]{1,0:T(8,128)S(1)}, s32[]{:T(128)}) %tuple.79), condition=%wide.region_6.6_spmd, body=%wide.region_5.5_spmd.sunk | while | flops 402784256 | bytes 2097213 | solution.py:26
  72.6 0.6 fusion.149
  74.2 0.6 fusion.149
  76.9 0.8 fusion.137
  77.7 1.9 reshape.35
  79.8 73.7 %all_to_all.34 = f32[4,32,8,512]{3,2,0,1:T(8,128)S(1)} all-to-all(f32[4,32,8,512]{3,2,0,1:T(8,128)S(1)} %copy.41), channel_id=1, replica_groups=mesh['energy'=32,'mom'=8] {'energy'}, dimensions={1} | all-to-all | bytes 4194304 | tf_op jit(solution)/shard_map/all_to_all | solution.py:78
  153.5 2.5 copy.42
  156.1 6.8 %all-to-all-start.1 = ((f32[128,8,512]{2,0,1:T(8,128)}), f32[128,8,512]{2,0,1:T(8,128)S(1)}, u32[]{:S(2)}, u32[]{:S(2)}) async-start(f32[128,8,512]{2,0,1:T(8,128)} %copy.42), calls=%async_computation.1 | async-start | bytes 4194304 | tf_op jit(solution)/shard_map/all_to_all | solution.py:79
  163.0 0.7 fusion.71
  163.9 24.9 %all-to-all-done.1 = f32[128,8,512]{2,0,1:T(8,128)S(1)} async-done(((f32[128,8,512]{2,0,1:T(8,128)}), f32[128,8,512]{2,0,1:T(8,128)S(1)}, u32[]{:S(2)}, u32[]{:S(2)}) %all-to-all-start.1) | async-done | bytes 2097184 | tf_op jit(solution)/shard_map/all_to_all | solution.py:79
  190.5 8.0 %fusion.20 = f32[128,8,512]{2,0,1:T(8,128)S(1)} fusion(f32[128,7,512]{2,0,1:T(8,128)S(1)} %get-tuple-element.180, f32[128,1,512]{2,0,1:T(8,128)S(1)} %get-tuple-element.182, f32[128,6,512]{2,0,1:T(8,128)S(1)} %get-tuple-element.184, f32[128,2,512]{2,0,1:T(8,128)S(1)} %get-tuple-element.186, f32[128,5,512]{2,0,1:T(8,128)S(1)} %get-tuple-element.188, ...), kind=kOutput, calls=%fused_computation.31 | convolution fusion | flops 817053696 | bytes 18875424 | tf_op jit(solution)/shard_map/ae,ekn->akn/dot_general | solution.py:85
  198.5 32.2 %all_to_all.35 = f32[128,8,512]{2,0,1:T(8,128)S(1)} all-to-all(f32[128,8,512]{2,0,1:T(8,128)S(1)} %fusion.20), channel_id=1, replica_groups=mesh['energy'=32,'mom'=8] {'mom'}, dimensions={1} | all-to-all | bytes 4194304 | tf_op jit(solution)/shard_map/all_to_all | solution.py:86
  230.7 1.2 copy.43
  231.9 56.4 %all_to_all.36 = f32[128,1,8,512]{3,2,1,0:T(8,128)S(1)} all-to-all(f32[128,1,8,512]{3,2,1,0:T(8,128)S(1)} %copy.43), channel_id=1, replica_groups=mesh['energy'=32,'mom'=8] {'energy'}, dimensions={0} | all-to-all | bytes 4194304 | tf_op jit(solution)/shard_map/all_to_all | solution.py:87
  288.6 1.5 copy.44
  290.1 2.9 mul.134
  293.0 3.2 %multiply_add_fusion = f32[4,1,2,256,256]{4,3,2,1,0:T(8,128)} fusion(f32[4,1,2,256,256]{4,3,2,1,0:T(8,128)} %mul.134, f32[4,1,2,256,256]{4,3,2,1,0:T(8,128)S(1)} %copy-done.1), kind=kLoop, calls=%fused_computation.53 | loop fusion | flops 1048576 | bytes 6291456 | tf_op jit(solution)/shard_map/add | solution.py:89
  (104 shorter events, 21.6 us)
Async XLA Ops:
  2.7 3.0 %copy-start = (f32[1,256,256]{2,1,0:T(8,128)S(1)}, f32[1,256,256]{2,1,0:T(8,128)}, u32[]{:S(2)}) copy-start(f32[1,256,256]{2,1,0:T(8,128)} %param.15) | copy-start | bytes 786436
  156.1 6.8 %copy-start.3 = (f32[16]{0:T(128)S(1)}, f32[16]{0:T(128)}, u32[]{:S(2)}) copy-start(f32[16]{0:T(128)} %param.18) | copy-start | bytes 196
  156.1 6.8 %copy-start.4 = (s32[16]{0:T(128)S(1)}, s32[16]{0:T(128)}, u32[]{:S(2)}) copy-start(s32[16]{0:T(128)} %param.19) | copy-start | bytes 196
  156.1 7.6 %copy-start.2 = (f32[128]{0:T(128)S(1)}, f32[128]{0:T(128)}, u32[]{:S(2)}) copy-start(f32[128]{0:T(128)} %param.16) | copy-start | bytes 1540
  156.1 32.7 %all-to-all-start.1 = ((f32[128,8,512]{2,0,1:T(8,128)}), f32[128,8,512]{2,0,1:T(8,128)S(1)}, u32[]{:S(2)}, u32[]{:S(2)}) async-start(f32[128,8,512]{2,0,1:T(8,128)} %copy.42), calls=%async_computation.1 | async-start | bytes 4194304 | tf_op jit(solution)/shard_map/all_to_all | solution.py:79
  290.1 2.9 copy-start.1
where the time goes:
time: 295 us; the launch traced here: 296 us
  blocking collectives  162 us (55%)
  matrix products  44 us (15%)
  local copies, waits for them, and re-layouts  25.5 us (9%)
  waiting for transfers between devices  24.9 us (8%)
  loops' own time  19.1 us (6%)
  other arithmetic  13.5 us (5%)
  starting transfers between devices  6.78 us (2%)
    all_to_all x1, blocking collectives, body(): lax.all_to_all(spread, 'energy', split_axis=1, concat_axis=0, tiled=True)  73.7 us
    all_to_all x1, blocking collectives, body(): lax.all_to_all(sigma_part[:, None], 'energy', split_axis=0, concat_axis=1...  56.4 us
    dot_general x60, matrix products, product(): jnp.dot(left_side, right_side, precision=PRECISE, preferred_element_type=...  36 us
    all_to_all x1, blocking collectives, body(): lax.all_to_all(folded, 'mom', split_axis=1, concat_axis=1, tiled=True)  32.2 us
    all_to_all x1, waiting for transfers between devices, body(): lax.all_to_all(column, 'mom', split_axis=1, concat_axis=1, tiled=True)  24.9 us
    another operation x8, loops' own time, invert(): lax.while_loop(keep_going, sweep, (jnp.int32(0), identity / energy))[1]  16.1 us
    dot_general x1, matrix products, body(): folded = jnp.einsum('ae,ekn->akn', kernel, mixed_rows, precision=PRECISE)  8 us
    all_to_all x1, starting transfers between devices, body(): lax.all_to_all(column, 'mom', split_axis=1, concat_axis=1, tiled=True)  6.78 us
  transfers between devices with their start and end apart: 1, of which 1 were waited for; matrix products, arithmetic and copies ran while one was open for 0% of the time, Pallas kernels for 0%

commit v1 on v0

v1 whole, which is shorter than its diff:
```python
import jax
import jax.numpy as jnp
from jax import lax
from jax.experimental import pallas as pl
from jax.experimental.pallas import tpu as pltpu
from jax.sharding import Mesh
from jax.sharding import PartitionSpec as P

MIX_RATE = 0.6
PHONON = 0.1
BROADENING = 0.02

M = 256
PTS = 4
E_TOT = 128
KN = 8
DEVS = 256
ROWS = 16
ORDER = ("xl", "xh", "y", "z", "c")
F32 = jnp.float32
BF16 = jnp.bfloat16
LIMIT = 58 * 1024 * 1024


def vmem():
    return pl.BlockSpec(memory_space=pltpu.VMEM)


def smem():
    return pl.BlockSpec(memory_space=pltpu.SMEM)


def split(x):
    high = x.astype(BF16)
    return high, (x - high.astype(F32)).astype(BF16)


def dot3(a, b):
    left = jnp.concatenate([a[0], a[0], a[1]], axis=1)
    right = jnp.concatenate([b[0], b[1], b[0]], axis=0)
    return jnp.dot(left, right, preferred_element_type=F32)


def both(top, bottom):
    return tuple(jnp.concatenate([t, b], axis=0) for t, b in zip(top, bottom))


def swap_halves(x, y):
    low = lax.broadcasted_iota(jnp.int32, x.shape, x.ndim - 2) < 4
    axis = x.ndim - 2
    first = jnp.where(low, x, pltpu.roll(y, 4, axis))
    second = jnp.where(low, pltpu.roll(x, 4, axis), y)
    return first, second


def invert_all(residuals, scales, slow):
    rows = lax.broadcasted_iota(jnp.int32, (M, M), 0)
    cols = lax.broadcasted_iota(jnp.int32, (M, M), 1)
    eye = (rows == cols).astype(F32)
    pairs = [split(r) for r in residuals]
    squares = [split(dot3(p, p)) for p in pairs]
    firsts = [(eye + r) * s for r, s in zip(residuals, scales)]
    stacked = [dot3(both(split(f), q), q) for f, q in zip(firsts, squares)]
    seconds = [f + s[:M] for f, s in zip(firsts, stacked)]
    fourths = [split(s[M:]) for s in stacked]
    stacked = [dot3(both(split(x), q), q) for x, q in zip(seconds, fourths)]
    thirds = [x + s[:M] for x, s in zip(seconds, stacked)]
    lasts = [x + dot3(split(x), split(s[M:])) for x, s in zip(thirds, stacked)]
    return [jnp.where(f, last, second) for f, last, second in zip(slow, lasts, seconds)]


def solve_kernel(sigma_ref, ham_ref, coup_ref, energy_ref, count_ref, out_ref, green_ref):
    rank = (lax.axis_index("xl") * 8 + lax.axis_index("z")) * 2 + lax.axis_index("c")
    coupling = split(coup_ref[...])
    turned = split(coup_ref[...].T)
    for group in range(2):
        points = (2 * group, 2 * group + 1)
        energy = [energy_ref[rank * PTS + p] for p in points]
        slow = [count_ref[rank * PTS + p] > 2 for p in points]
        scale = [1.0 / jnp.full((M, M), e, F32) for e in energy]
        residual = [(ham_ref[:M] + sigma_ref[p, :M]) * s for p, s in zip(points, scale)]
        left = invert_all(residual, scale, slow)
        inverse = [split(x) for x in left]
        coupled = [split(dot3(x, coupling)) for x in inverse]
        back = [split(dot3(turned, x)) for x in inverse]
        residual = [
            (ham_ref[M:] + sigma_ref[p, M:] + dot3(turned, c)) * s
            for p, c, s in zip(points, coupled, scale)
        ]
        right = invert_all(residual, scale, slow)
        through = [split(dot3(c, split(r))) for c, r in zip(coupled, right)]
        for i in range(2):
            green_ref[i, :M] = left[i] + dot3(through[i], back[i])
            green_ref[i, M:] = right[i]
        for block in range(8):
            slab = slice(block * 64, block * 64 + 64)
            first = green_ref[0, slab].reshape(8, 8, M)
            second = green_ref[1, slab].reshape(8, 8, M)
            for parity, tiles in enumerate(swap_halves(first, second)):
                for t in range(8):
                    for half in range(2):
                        piece = block * 32 + 4 * t + 2 * parity + half
                        lanes = slice(half * 128, half * 128 + 128)
                        out_ref[piece, group * 8 : group * 8 + 8] = tiles[t, :, lanes]


def solve(sigma, ham, coupling, energies, counts):
    return pl.pallas_call(
        solve_kernel,
        out_shape=jax.ShapeDtypeStruct((DEVS, ROWS, 128), F32),
        in_specs=[vmem(), vmem(), vmem(), smem(), smem()],
        out_specs=vmem(),
        scratch_shapes=[pltpu.VMEM((2, 2 * M, M), F32)],
        compiler_params=pltpu.CompilerParams(vmem_limit_bytes=LIMIT),
        cost_estimate=pl.CostEstimate(flops=6_800_000_000, bytes_accessed=5_000_000, transcendentals=0),
        name="solve_points",
    )(sigma, ham, coupling, energies, counts)


def lorentz(offset):
    scaled = offset / BROADENING
    return 1.0 / (1.0 + scaled * scaled)


def operator_kernel(energy_ref, strength_ref, offset_ref, high_ref, low_ref, weight_ref):
    columns = jnp.broadcast_to(energy_ref[...], (E_TOT, E_TOT))
    spacing = columns.T - columns
    values = lorentz(spacing - PHONON) + lorentz(spacing + PHONON)
    values = values / jnp.sum(values, axis=1, keepdims=True)
    wide = E_TOT * 4
    spread = (
        lax.broadcasted_iota(jnp.int32, (wide, E_TOT), 0) // 4
        == lax.broadcasted_iota(jnp.int32, (wide, E_TOT), 1)
    ).astype(BF16)
    gather = (
        lax.broadcasted_iota(jnp.int32, (E_TOT, wide), 1) // 4
        == lax.broadcasted_iota(jnp.int32, (E_TOT, wide), 0)
    ).astype(BF16)
    row_id = lax.broadcasted_iota(jnp.int32, (wide, wide), 0)
    col_id = lax.broadcasted_iota(jnp.int32, (wide, wide), 1)
    same = ((row_id ^ col_id) & 3) == 0
    for part, ref in zip(split(values), (high_ref, low_ref)):
        tall = jnp.dot(spread, part, preferred_element_type=F32).astype(BF16)
        full = jnp.dot(tall, gather, preferred_element_type=F32)
        ref[...] = jnp.where(same, full, 0.0).astype(BF16)
    for d in range(KN):
        total = jnp.float32(0.0)
        for j in range(16):
            total = total + jnp.where(offset_ref[j] == d, strength_ref[j], 0.0)
        weight_ref[d] = total


def build_operator(energies, strengths, offsets):
    return pl.pallas_call(
        operator_kernel,
        out_shape=[
            jax.ShapeDtypeStruct((512, 512), BF16),
            jax.ShapeDtypeStruct((512, 512), BF16),
            jax.ShapeDtypeStruct((KN,), F32),
        ],
        in_specs=[vmem(), smem(), smem()],
        out_specs=[vmem(), vmem(), smem()],
        compiler_params=pltpu.CompilerParams(vmem_limit_bytes=16 * 1024 * 1024),
        cost_estimate=pl.CostEstimate(flops=150_000_000, bytes_accessed=1_500_000, transcendentals=0),
        name="energy_operator",
    )(energies, strengths, offsets)


def mix_kernel(high_ref, low_ref, weight_ref, in_ref, out_ref, x_high, x_low):
    weight = [weight_ref[d] for d in range(KN)]
    for upper in range(2):
        for device in range(16):
            given = [in_ref[(upper * KN + k) * 16 + device] for k in range(KN)]
            row = (upper * 16 + device) * ROWS
            for k in range(KN):
                total = weight[0] * given[k]
                for s in range(1, KN):
                    total = total + weight[s] * given[(k - s) % KN]
                high, low = split(total)
                x_high[row : row + ROWS, k * 128 : k * 128 + 128] = high
                x_low[row : row + ROWS, k * 128 : k * 128 + 128] = low
    left = jnp.concatenate([high_ref[...], high_ref[...], low_ref[...]], axis=1)
    for pair in range(KN // 2):
        lanes = slice(pair * 256, pair * 256 + 256)
        right = jnp.concatenate([x_high[:, lanes], x_low[:, lanes], x_high[:, lanes]], axis=0)
        mixed = jnp.dot(left, right, preferred_element_type=F32)
        for k in (2 * pair, 2 * pair + 1):
            part = mixed[:, (k % 2) * 128 : (k % 2) * 128 + 128].reshape(32, ROWS, 128)
            for upper in range(2):
                first = (upper * KN + k) * 16
                out_ref[first : first + 16] = part[upper * 16 : upper * 16 + 16]


def mix(operator, x):
    return pl.pallas_call(
        mix_kernel,
        out_shape=jax.ShapeDtypeStruct((DEVS, ROWS, 128), F32),
        in_specs=[vmem(), vmem(), smem(), vmem()],
        out_specs=vmem(),
        scratch_shapes=[pltpu.VMEM((512, 1024), BF16), pltpu.VMEM((512, 1024), BF16)],
        compiler_params=pltpu.CompilerParams(vmem_limit_bytes=24 * 1024 * 1024),
        cost_estimate=pl.CostEstimate(flops=1_600_000_000, bytes_accessed=5_000_000, transcendentals=0),
        name="mix_energies",
    )(*operator, x)


def blend_kernel(sigma_ref, in_ref, out_ref):
    for t in range(16):
        rows = slice(8 * t, 8 * t + 8)
        for half in range(2):
            lanes = slice(half * 128, half * 128 + 128)
            even = in_ref[4 * t + half]
            odd = in_ref[4 * t + 2 + half]
            tiles = swap_halves(even[:8], odd[:8]) + swap_halves(even[8:], odd[8:])
            for p, tile in enumerate(tiles):
                old = sigma_ref[p, rows, lanes]
                out_ref[p, rows, lanes] = (1.0 - MIX_RATE) * old + MIX_RATE * tile


def blend(sigma, x):
    steps = 4
    rows = 2 * M // steps
    return pl.pallas_call(
        blend_kernel,
        out_shape=jax.ShapeDtypeStruct((PTS, 2 * M, M), F32),
        grid=(steps,),
        in_specs=[
            pl.BlockSpec((PTS, rows, M), lambda i: (0, i, 0)),
            pl.BlockSpec((DEVS // steps, ROWS, 128), lambda i: (i, 0, 0)),
        ],
        out_specs=pl.BlockSpec((PTS, rows, M), lambda i: (0, i, 0)),
        compiler_params=pltpu.CompilerParams(vmem_limit_bytes=16 * 1024 * 1024),
        cost_estimate=pl.CostEstimate(flops=2_000_000, bytes_accessed=6_000_000, transcendentals=0),
        name="blend_old",
    )(sigma, x)


def exchange(x):
    return lax.all_to_all(x, ORDER, split_axis=0, concat_axis=0, tiled=True)


def body(sigma_in, hamiltonian, coupling, energies, counts, strengths, offsets):
    sigma = sigma_in.reshape(PTS, 2 * M, M)
    green = solve(sigma, hamiltonian.reshape(2 * M, M), coupling.reshape(M, M), energies, counts)
    columns = exchange(green)
    operator = build_operator(energies.reshape(1, E_TOT), strengths, offsets)
    result = exchange(mix(operator, columns))
    return blend(sigma, result).reshape(sigma_in.shape)


def solution(mesh):
    fine = Mesh(mesh.devices.reshape(2, 8, 2, 2, 4), ("xl", "z", "c", "xh", "y"))
    energy, mom = ("xl", "z", "c"), ("xh", "y")
    return jax.shard_map(
        body,
        mesh=fine,
        in_specs=(
            P(energy, mom, None, None, None),
            P(mom, None, None, None),
            P(mom, None, None),
            P(),
            P(),
            P(),
            P(),
        ),
        out_specs=P(energy, mom, None, None, None),
        check_vma=False,
    )
```

time: 295 us -> 147 us (0.50)
  blocking collectives: 162 us -> 59.3 us
  matrix products: 44 us -> 0 us
  waiting for transfers between devices: 24.9 us -> 51.1 us
  local copies, waits for them, and re-layouts: 25.5 us -> 0.02 us
  Pallas kernels: 0 us -> 20.6 us
  loops' own time: 19.1 us -> 0 us
  other arithmetic: 13.5 us -> 0 us
  starting transfers between devices: 6.78 us -> 15.7 us
    all_to_all x3 -> x1, blocking collectives: 162 us -> 59.3 us  [exchange(): return lax.all_to_all(x, ORDER, split_axis=0, concat_axis=0, tiled=True)]
    dot_general x61 -> x0, matrix products: 44 us -> none  [the longest x60 36 us: product(): jnp.dot(left_side, right_side, precision=PRECISE, preferred_element_type=...]
    all_to_all x1, waiting for transfers between devices: 24.9 us -> 51.1 us  [exchange(): return lax.all_to_all(x, ORDER, split_axis=0, concat_axis=0, tiled=True)]
    pallas_call x0 -> x4, Pallas kernels: none -> 20.6 us  [the longest x1 12.9 us: solve(): pl.pallas_call(solve_kernel, out_shape=jax.ShapeDtypeStruct((DEVS, ROWS,...]
    another operation x9 -> x0, loops' own time: 19.1 us -> none  [the longest x8 16.1 us: invert(): lax.while_loop(keep_going, sweep, (jnp.int32(0), identity / energy))[1]]
    all_to_all x1, starting transfers between devices: 6.78 us -> 15.7 us  [exchange(): return lax.all_to_all(x, ORDER, split_axis=0, concat_axis=0, tiled=True)]
    sub x4 -> x0, other arithmetic: 6.37 us -> none  [solve_point(): left_matrix = energy * identity - ham_block[0] - sigma_pair[0]]
    dynamic_slice x10 -> x0, local copies, waits for them, and re-layouts: 6.13 us -> none  [the longest x8 4.68 us: body(): green_blocks = lax.map(solve_held, (blocks, own_energy, own_count))]
  transfers between devices with their start and end apart: 1 -> 1, of which waited for: 1 -> 1; matrix products, arithmetic and copies ran while one was open for 0% -> 0% of each run, Pallas kernels for 0% -> 2%
where the time goes in v1:
time: 147 us
  blocking collectives  59.3 us (40%)
  waiting for transfers between devices  51.1 us (35%)
  Pallas kernels  20.6 us (14%)
  starting transfers between devices  15.7 us (11%)
    all_to_all x1, blocking collectives, exchange(): return lax.all_to_all(x, ORDER, split_axis=0, concat_axis=0, tiled=True)  59.3 us
    all_to_all x1, waiting for transfers between devices, exchange(): return lax.all_to_all(x, ORDER, split_axis=0, concat_axis=0, tiled=True)  51.1 us
    all_to_all x1, starting transfers between devices, exchange(): return lax.all_to_all(x, ORDER, split_axis=0, concat_axis=0, tiled=True)  15.7 us
    pallas_call x1, Pallas kernels, solve(): pl.pallas_call(solve_kernel, out_shape=jax.ShapeDtypeStruct((DEVS, ROWS,...  12.9 us
    pallas_call x1, Pallas kernels, mix(): pl.pallas_call(mix_kernel, out_shape=jax.ShapeDtypeStruct((DEVS, ROWS, 12...  3.4 us
  transfers between devices with their start and end apart: 1, of which 1 were waited for; matrix products, arithmetic and copies ran while one was open for 0% of the time, Pallas kernels for 2%

profile of v1, /device:TPU:1, one launch (start us, length us, event | category | flops | bytes accessed | tf_op | source)
XLA Modules:
  0.0 146.7 jit_solution(17268527426198739934)
XLA Ops:
  0.0 12.9 %solve_points.1 = f32[256,16,128]{2,1,0:T(8,128)} custom-call(f32[4,512,256]{2,1,0:T(8,128)} %bitcast.7, f32[512,256]{1,0:T(8,128)} %bitcast.10, f32[256,256]{1,0:T(8,128)} %bitcast.11, f32[128]{0:T(128)} %energy_ref.1, s32[128]{0:T(128)} %count_ref.1), custom_call_target="tpu_custom_call" | custom-call | flops 6800000000 | bytes 5000000 | tf_op jit(solution)/shard_map/solve_points/pallas_call | solution.py:108
  12.9 0.0 copy-start.1
  12.9 0.0 copy-start.2
  12.9 0.0 copy-start.3
  12.9 15.7 %all-to-all-start = ((f32[256,16,128]{2,1,0:T(8,128)}), f32[256,16,128]{2,1,0:T(8,128)S(1)}, u32[]{:S(2)}, u32[]{:S(2)}) async-start(f32[256,16,128]{2,1,0:T(8,128)} %solve_points.1), calls=%async_computation | async-start | bytes 4194304 | tf_op jit(solution)/shard_map/all_to_all | solution.py:239
  28.6 0.0 copy-done.1
  28.6 0.0 copy-done.2
  28.6 0.0 copy-done.3
  28.6 2.2 %energy_operator.1 = (bf16[512,512]{1,0:T(8,128)(2,1)S(1)}, bf16[512,512]{1,0:T(8,128)(2,1)S(1)}, f32[8]{0:T(128)S(1)}) custom-call(f32[1,128]{1,0:T(1,128)S(1)} %bitcast.9, f32[16]{0:T(128)S(1)} %copy-done.2, s32[16]{0:T(128)S(1)} %copy-done.3), custom_call_target="tpu_custom_call" | custom-call | flops 150000000 | bytes 1500000 | tf_op jit(solution)/shard_map/energy_operator/pallas_call | solution.py:154
  30.8 51.1 %all-to-all-done.in_ref = f32[256,16,128]{2,1,0:T(8,128)S(1)} async-done(((f32[256,16,128]{2,1,0:T(8,128)}), f32[256,16,128]{2,1,0:T(8,128)S(1)}, u32[]{:S(2)}, u32[]{:S(2)}) %all-to-all-start) | async-done | bytes 2097184 | tf_op jit(solution)/shard_map/all_to_all | solution.py:239
  81.9 3.4 %mix_energies.1 = f32[256,16,128]{2,1,0:T(8,128)S(1)} custom-call(bf16[512,512]{1,0:T(8,128)(2,1)S(1)} %get-tuple-element.8.high_ref, bf16[512,512]{1,0:T(8,128)(2,1)S(1)} %get-tuple-element.9.low_ref, f32[8]{0:T(128)S(1)} %get-tuple-element.10.weight_ref, f32[256,16,128]{2,1,0:T(8,128)S(1)} %all-to-all-done.in_ref), custom_call_target="tpu_custom_call" | custom-call | flops 1600000000 | bytes 5000000 | tf_op jit(solution)/shard_map/mix_energies/pallas_call | solution.py:195
  85.3 0.0 copy-start
  85.3 59.3 %all_to_all.10.in_ref = f32[256,16,128]{2,1,0:T(8,128)S(1)} all-to-all(f32[256,16,128]{2,1,0:T(8,128)S(1)} %mix_energies.1), channel_id=1, replica_groups=mesh['xl'=2,'z'=8,'c'=2,'xh'=2,'y'=4] {'xl','xh','y','z','c'}, dimensions={0} | all-to-all | bytes 4194304 | tf_op jit(solution)/shard_map/all_to_all | solution.py:239
  144.6 0.0 copy-done
  144.6 2.1 %blend_old.1 = f32[4,512,256]{2,1,0:T(8,128)} custom-call(f32[4,512,256]{2,1,0:T(8,128)S(1)} %bitcast.8, f32[256,16,128]{2,1,0:T(8,128)S(1)} %all_to_all.10.in_ref), custom_call_target="tpu_custom_call" | custom-call | flops 2000000 | bytes 6000000 | tf_op jit(solution)/shard_map/blend_old/pallas_call | solution.py:223
Async XLA Ops:
  12.9 15.7 %copy-start.1 = (f32[128]{0:T(128)S(1)}, f32[128]{0:T(128)}, u32[]{:S(2)}) copy-start(f32[128]{0:T(128)} %energy_ref.1) | copy-start | bytes 1540
  12.9 15.7 %copy-start.2 = (f32[16]{0:T(128)S(1)}, f32[16]{0:T(128)}, u32[]{:S(2)}) copy-start(f32[16]{0:T(128)} %strength_ref.1) | copy-start | bytes 196
  12.9 15.7 %copy-start.3 = (s32[16]{0:T(128)S(1)}, s32[16]{0:T(128)}, u32[]{:S(2)}) copy-start(s32[16]{0:T(128)} %offset_ref.1) | copy-start | bytes 196
  12.9 69.0 %all-to-all-start = ((f32[256,16,128]{2,1,0:T(8,128)}), f32[256,16,128]{2,1,0:T(8,128)S(1)}, u32[]{:S(2)}, u32[]{:S(2)}) async-start(f32[256,16,128]{2,1,0:T(8,128)} %solve_points.1), calls=%async_computation | async-start | bytes 4194304 | tf_op jit(solution)/shard_map/all_to_all | solution.py:239
  85.3 59.3 %copy-start = (f32[4,1,2,256,256]{4,3,2,1,0:T(8,128)S(1)}, f32[4,1,2,256,256]{4,3,2,1,0:T(8,128)}, u32[]{:S(2)}) copy-start(f32[4,1,2,256,256]{4,3,2,1,0:T(8,128)} %param.7) | copy-start | bytes 6291460

commit v2 on v1

v2 whole, which is shorter than its diff:
```python
import jax
import jax.numpy as jnp
from jax import lax
from jax.experimental import pallas as pl
from jax.experimental.pallas import tpu as pltpu
from jax.sharding import Mesh
from jax.sharding import PartitionSpec as P

MIX_RATE = 0.6
PHONON = 0.1
BROADENING = 0.02

M = 256
PTS = 4
E_TOT = 128
KN = 8
DEVS = 256
ROWS = 16
ORDER = ("xl", "xh", "y", "z", "c")
F32 = jnp.float32
BF16 = jnp.bfloat16


def vmem():
    return pl.BlockSpec(memory_space=pltpu.VMEM)


def smem():
    return pl.BlockSpec(memory_space=pltpu.SMEM)


def split(x):
    high = x.astype(BF16)
    return high, (x - high.astype(F32)).astype(BF16)


def dot3(a, b):
    left = jnp.concatenate([a[0], a[0], a[1]], axis=1)
    right = jnp.concatenate([b[0], b[1], b[0]], axis=0)
    return jnp.dot(left, right, preferred_element_type=F32)


def both(top, bottom):
    return tuple(jnp.concatenate([t, b], axis=0) for t, b in zip(top, bottom))


def swap_halves(x, y):
    low = lax.broadcasted_iota(jnp.int32, x.shape, x.ndim - 2) < 4
    axis = x.ndim - 2
    first = jnp.where(low, x, pltpu.roll(y, 4, axis))
    second = jnp.where(low, pltpu.roll(x, 4, axis), y)
    return first, second


def invert_all(residuals, scales, slow):
    rows = lax.broadcasted_iota(jnp.int32, (M, M), 0)
    cols = lax.broadcasted_iota(jnp.int32, (M, M), 1)
    eye = (rows == cols).astype(F32)
    pairs = [split(r) for r in residuals]
    squares = [split(dot3(p, p)) for p in pairs]
    firsts = [(eye + r) * s for r, s in zip(residuals, scales)]
    stacked = [dot3(both(split(f), q), q) for f, q in zip(firsts, squares)]
    seconds = [f + s[:M] for f, s in zip(firsts, stacked)]
    fourths = [split(s[M:]) for s in stacked]
    stacked = [dot3(both(split(x), q), q) for x, q in zip(seconds, fourths)]
    thirds = [x + s[:M] for x, s in zip(seconds, stacked)]
    lasts = [x + dot3(split(x), split(s[M:])) for x, s in zip(thirds, stacked)]
    return [jnp.where(f, last, second) for f, last, second in zip(slow, lasts, seconds)]


def to_pieces(green, out_ref, base):
    for block in range(4):
        slab = slice(block * 64, block * 64 + 64)
        for group in range(2):
            first = green[2 * group][slab].reshape(8, 8, M)
            second = green[2 * group + 1][slab].reshape(8, 8, M)
            for parity, tiles in enumerate(swap_halves(first, second)):
                for t in range(8):
                    for half in range(2):
                        piece = base + block * 32 + 4 * t + 2 * parity + half
                        lanes = slice(half * 128, half * 128 + 128)
                        out_ref[piece, group * 8 : group * 8 + 8] = tiles[t, :, lanes]


def solve_kernel(
    sigma_hbm,
    ham_hbm,
    coup_hbm,
    energy_ref,
    count_ref,
    out_hbm,
    out_ref,
    sigma_ref,
    ham_ref,
    coup_ref,
    sems,
):
    upper, lower = pl.ds(0, M), pl.ds(M, M)
    copies = [
        pltpu.make_async_copy(ham_hbm.at[upper], ham_ref.at[upper], sems.at[0]),
        *(
            pltpu.make_async_copy(sigma_hbm.at[p, upper], sigma_ref.at[p, upper], sems.at[1 + p])
            for p in range(PTS)
        ),
        pltpu.make_async_copy(coup_hbm, coup_ref, sems.at[5]),
        pltpu.make_async_copy(ham_hbm.at[lower], ham_ref.at[lower], sems.at[6]),
        pltpu.make_async_copy(sigma_hbm.at[:, lower], sigma_ref.at[:, lower], sems.at[7]),
    ]
    for copy in copies:
        copy.start()
    rank = (lax.axis_index("xl") * 8 + lax.axis_index("z")) * 2 + lax.axis_index("c")
    points = range(PTS)
    energy = [energy_ref[rank * PTS + p] for p in points]
    slow = [count_ref[rank * PTS + p] > 2 for p in points]
    scale = [1.0 / jnp.full((M, M), e, F32) for e in energy]
    copies[0].wait()
    residual = []
    for p in points:
        copies[1 + p].wait()
        residual.append((ham_ref[:M] + sigma_ref[p, :M]) * scale[p])
    left = invert_all(residual, scale, slow)
    for copy in copies[5:]:
        copy.wait()
    coupling = split(coup_ref[...])
    turned = split(coup_ref[...].T)
    inverse = [split(x) for x in left]
    coupled = [split(dot3(x, coupling)) for x in inverse]
    back = [split(dot3(turned, x)) for x in inverse]
    residual = [
        (ham_ref[M:] + sigma_ref[p, M:] + dot3(turned, coupled[p])) * scale[p] for p in points
    ]
    right = invert_all(residual, scale, slow)
    to_pieces(right, out_ref, 128)
    half = pl.ds(128, 128)
    sent = pltpu.make_async_copy(out_ref.at[half], out_hbm.at[half], sems.at[8])
    sent.start()
    through = [split(dot3(c, split(r))) for c, r in zip(coupled, right)]
    to_pieces([x + dot3(t, b) for x, t, b in zip(left, through, back)], out_ref, 0)
    half = pl.ds(0, 128)
    last = pltpu.make_async_copy(out_ref.at[half], out_hbm.at[half], sems.at[9])
    last.start()
    sent.wait()
    last.wait()


def solve(sigma, ham, coupling, energies, counts):
    hbm = pl.BlockSpec(memory_space=pltpu.HBM)
    return pl.pallas_call(
        solve_kernel,
        out_shape=jax.ShapeDtypeStruct((DEVS, ROWS, 128), F32),
        in_specs=[hbm, hbm, hbm, smem(), smem()],
        out_specs=hbm,
        scratch_shapes=[
            pltpu.VMEM((DEVS, ROWS, 128), F32),
            pltpu.VMEM((PTS, 2 * M, M), F32),
            pltpu.VMEM((2 * M, M), F32),
            pltpu.VMEM((M, M), F32),
            pltpu.SemaphoreType.DMA((10,)),
        ],
        compiler_params=pltpu.CompilerParams(vmem_limit_bytes=60 * 1024 * 1024),
        cost_estimate=pl.CostEstimate(flops=6_800_000_000, bytes_accessed=5_000_000, transcendentals=0),
        name="solve_points",
    )(sigma, ham, coupling, energies, counts)


def lorentz(offset):
    scaled = offset / BROADENING
    return 1.0 / (1.0 + scaled * scaled)


def energy_operator(energies):
    columns = jnp.broadcast_to(energies, (E_TOT, E_TOT))
    spacing = columns.T - columns
    values = lorentz(spacing - PHONON) + lorentz(spacing + PHONON)
    values = values / jnp.sum(values, axis=1, keepdims=True)
    wide = E_TOT * 4
    spread = (
        lax.broadcasted_iota(jnp.int32, (wide, E_TOT), 0) // 4
        == lax.broadcasted_iota(jnp.int32, (wide, E_TOT), 1)
    ).astype(BF16)
    gather = (
        lax.broadcasted_iota(jnp.int32, (E_TOT, wide), 1) // 4
        == lax.broadcasted_iota(jnp.int32, (E_TOT, wide), 0)
    ).astype(BF16)
    row_id = lax.broadcasted_iota(jnp.int32, (wide, wide), 0)
    col_id = lax.broadcasted_iota(jnp.int32, (wide, wide), 1)
    same = ((row_id ^ col_id) & 3) == 0
    parts = []
    for part in split(values):
        tall = jnp.dot(spread, part, preferred_element_type=F32).astype(BF16)
        full = jnp.dot(tall, gather, preferred_element_type=F32)
        parts.append(jnp.where(same, full, 0.0).astype(BF16))
    return parts


def mix_kernel(energy_ref, strength_ref, offset_ref, in_ref, out_ref, high_ref, low_ref, x_high, x_low):
    weight = []
    for d in range(KN):
        total = jnp.float32(0.0)
        for j in range(16):
            total = total + jnp.where(offset_ref[j] == d, strength_ref[j], 0.0)
        weight.append(total)
    high_ref[...], low_ref[...] = energy_operator(energy_ref[...])
    for pair in range(KN // 2):
        targets = (2 * pair, 2 * pair + 1)
        for upper in range(2):
            for device in range(16):
                given = [in_ref[(upper * KN + k) * 16 + device] for k in range(KN)]
                row = (upper * 16 + device) * ROWS
                for k in targets:
                    total = weight[0] * given[k]
                    for s in range(1, KN):
                        total = total + weight[s] * given[(k - s) % KN]
                    high, low = split(total)
                    x_high[row : row + ROWS, k * 128 : k * 128 + 128] = high
                    x_low[row : row + ROWS, k * 128 : k * 128 + 128] = low
        lanes = slice(pair * 256, pair * 256 + 256)
        high, low = high_ref[...], low_ref[...]
        left = jnp.concatenate([high, high, low], axis=1)
        right = jnp.concatenate([x_high[:, lanes], x_low[:, lanes], x_high[:, lanes]], axis=0)
        mixed = jnp.dot(left, right, preferred_element_type=F32)
        for k in targets:
            part = mixed[:, (k % 2) * 128 : (k % 2) * 128 + 128].reshape(32, ROWS, 128)
            for upper in range(2):
                first = (upper * KN + k) * 16
                out_ref[first : first + 16] = part[upper * 16 : upper * 16 + 16]


def mix(energies, strengths, offsets, x):
    return pl.pallas_call(
        mix_kernel,
        out_shape=jax.ShapeDtypeStruct((DEVS, ROWS, 128), F32),
        in_specs=[vmem(), smem(), smem(), vmem()],
        out_specs=vmem(),
        scratch_shapes=[
            pltpu.VMEM((512, 512), BF16),
            pltpu.VMEM((512, 512), BF16),
            pltpu.VMEM((512, 1024), BF16),
            pltpu.VMEM((512, 1024), BF16),
        ],
        compiler_params=pltpu.CompilerParams(vmem_limit_bytes=32 * 1024 * 1024),
        cost_estimate=pl.CostEstimate(flops=1_700_000_000, bytes_accessed=4_200_000, transcendentals=0),
        name="mix_energies",
    )(energies, strengths, offsets, x)


def blend_kernel(sigma_ref, in_ref, out_hbm, out_ref, sems):
    copies = []
    for block in range(4):
        for t in range(16 * block, 16 * block + 16):
            rows = slice(8 * t, 8 * t + 8)
            for half in range(2):
                lanes = slice(half * 128, half * 128 + 128)
                even = in_ref[4 * t + half]
                odd = in_ref[4 * t + 2 + half]
                tiles = swap_halves(even[:8], odd[:8]) + swap_halves(even[8:], odd[8:])
                for p, tile in enumerate(tiles):
                    old = sigma_ref[p, rows, lanes]
                    out_ref[p, rows, lanes] = (1.0 - MIX_RATE) * old + MIX_RATE * tile
        rows = pl.ds(128 * block, 128)
        copies.append(
            pltpu.make_async_copy(out_ref.at[:, rows], out_hbm.at[:, rows], sems.at[block])
        )
        copies[-1].start()
    for copy in copies:
        copy.wait()


def blend(sigma, x):
    return pl.pallas_call(
        blend_kernel,
        out_shape=jax.ShapeDtypeStruct((PTS, 2 * M, M), F32),
        in_specs=[vmem(), vmem()],
        out_specs=pl.BlockSpec(memory_space=pltpu.HBM),
        scratch_shapes=[pltpu.VMEM((PTS, 2 * M, M), F32), pltpu.SemaphoreType.DMA((4,))],
        compiler_params=pltpu.CompilerParams(vmem_limit_bytes=24 * 1024 * 1024),
        cost_estimate=pl.CostEstimate(flops=2_000_000, bytes_accessed=6_000_000, transcendentals=0),
        name="blend_old",
    )(sigma, x)


def exchange(x):
    return lax.all_to_all(x, ORDER, split_axis=0, concat_axis=0, tiled=True)


def body(sigma_in, hamiltonian, coupling, energies, counts, strengths, offsets):
    sigma = sigma_in.reshape(PTS, 2 * M, M)
    green = solve(sigma, hamiltonian.reshape(2 * M, M), coupling.reshape(M, M), energies, counts)
    columns = exchange(green)
    mixed = mix(energies.reshape(1, E_TOT), strengths, offsets, columns)
    result = exchange(mixed)
    return blend(sigma, result).reshape(sigma_in.shape)


def solution(mesh):
    fine = Mesh(mesh.devices.reshape(2, 8, 2, 2, 4), ("xl", "z", "c", "xh", "y"))
    energy, mom = ("xl", "z", "c"), ("xh", "y")
    return jax.shard_map(
        body,
        mesh=fine,
        in_specs=(
            P(energy, mom, None, None, None),
            P(mom, None, None, None),
            P(mom, None, None),
            P(),
            P(),
            P(),
            P(),
        ),
        out_specs=P(energy, mom, None, None, None),
        check_vma=False,
    )
```

time: 147 us -> 145 us (0.986)
  blocking collectives: 59.3 us -> 128 us
  waiting for transfers between devices: 51.1 us -> 0 us
  starting transfers between devices: 15.7 us -> 0 us
  Pallas kernels: 20.6 us -> 16.3 us
    all_to_all x1 -> x2, blocking collectives: 59.3 us -> 128 us  [exchange(): return lax.all_to_all(x, ORDER, split_axis=0, concat_axis=0, tiled=True)]
    all_to_all x1 -> x0, waiting for transfers between devices: 51.1 us -> none  [exchange(): return lax.all_to_all(x, ORDER, split_axis=0, concat_axis=0, tiled=True)]
    all_to_all x1 -> x0, starting transfers between devices: 15.7 us -> none  [exchange(): return lax.all_to_all(x, ORDER, split_axis=0, concat_axis=0, tiled=True)]
    pallas_call x1, Pallas kernels: 12.9 us -> 10.7 us  [solve(): pl.pallas_call(solve_kernel, out_shape=jax.ShapeDtypeStruct((DEVS, ROWS,...]
    pallas_call x1 -> x0, Pallas kernels: 2.2 us -> none  [build_operator(): pl.pallas_call(operator_kernel, out_shape=[jax.ShapeDtypeStruct((512, 512...]
  transfers between devices with their start and end apart: 1 -> 0, of which waited for: 1 -> 0; matrix products, arithmetic and copies ran while one was open for 0% -> 0% of each run, Pallas kernels for 2% -> 0%
where the time goes in v2:
time: 145 us
  blocking collectives  128 us (88%)
  Pallas kernels  16.3 us (11%)
    all_to_all x2, blocking collectives, exchange(): return lax.all_to_all(x, ORDER, split_axis=0, concat_axis=0, tiled=True)  128 us
    pallas_call x1, Pallas kernels, solve(): pl.pallas_call(solve_kernel, out_shape=jax.ShapeDtypeStruct((DEVS, ROWS,...  10.7 us
    pallas_call x1, Pallas kernels, mix(): pl.pallas_call(mix_kernel, out_shape=jax.ShapeDtypeStruct((DEVS, ROWS, 12...  4.16 us

profile of v2, /device:TPU:1, one launch (start us, length us, event | category | flops | bytes accessed | tf_op | source)
XLA Modules:
  0.0 144.6 jit_solution(16512228698628773285)
XLA Ops:
  0.0 10.7 %solve_points.1 = f32[256,16,128]{2,1,0:T(8,128)} custom-call(f32[4,512,256]{2,1,0:T(8,128)} %bitcast.7, f32[512,256]{1,0:T(8,128)} %bitcast.10, f32[256,256]{1,0:T(8,128)} %bitcast.11, f32[128]{0:T(128)} %energy_ref.1, s32[128]{0:T(128)} %count_ref.1), custom_call_target="tpu_custom_call" | custom-call | flops 6800000000 | bytes 5000000 | tf_op jit(solution)/shard_map/solve_points/pallas_call | solution.py:148
  10.7 0.0 copy-start.1
  10.7 0.0 copy-start.2
  10.7 0.0 copy-start.3
  10.7 69.0 %all_to_all.10.in_ref = f32[256,16,128]{2,1,0:T(8,128)S(1)} all-to-all(f32[256,16,128]{2,1,0:T(8,128)} %solve_points.1), channel_id=1, replica_groups=mesh['xl'=2,'z'=8,'c'=2,'xh'=2,'y'=4] {'xl','xh','y','z','c'}, dimensions={0} | all-to-all | bytes 4194304 | tf_op jit(solution)/shard_map/all_to_all | solution.py:283
  79.7 0.0 copy-done.1
  79.7 0.0 copy-done.2
  79.7 0.0 copy-done.3
  79.7 4.2 %mix_energies.1 = f32[256,16,128]{2,1,0:T(8,128)S(1)} custom-call(f32[1,128]{1,0:T(1,128)S(1)} %bitcast.9, f32[16]{0:T(128)S(1)} %copy-done.2, s32[16]{0:T(128)S(1)} %copy-done.3, f32[256,16,128]{2,1,0:T(8,128)S(1)} %all_to_all.10.in_ref), custom_call_target="tpu_custom_call" | custom-call | flops 1700000000 | bytes 4200000 | tf_op jit(solution)/shard_map/mix_energies/pallas_call | solution.py:230
  83.9 0.0 copy-start
  83.9 59.3 %all_to_all.11.in_ref = f32[256,16,128]{2,1,0:T(8,128)S(1)} all-to-all(f32[256,16,128]{2,1,0:T(8,128)S(1)} %mix_energies.1), channel_id=1, replica_groups=mesh['xl'=2,'z'=8,'c'=2,'xh'=2,'y'=4] {'xl','xh','y','z','c'}, dimensions={0} | all-to-all | bytes 4194304 | tf_op jit(solution)/shard_map/all_to_all | solution.py:283
  143.2 0.0 copy-done
  143.2 1.4 blend_old.1
Async XLA Ops:
  10.7 69.1 %copy-start.1 = (f32[128]{0:T(128)S(1)}, f32[128]{0:T(128)}, u32[]{:S(2)}) copy-start(f32[128]{0:T(128)} %energy_ref.1) | copy-start | bytes 1540
  10.7 69.1 %copy-start.2 = (f32[16]{0:T(128)S(1)}, f32[16]{0:T(128)}, u32[]{:S(2)}) copy-start(f32[16]{0:T(128)} %strength_ref.1) | copy-start | bytes 196
  10.7 69.0 %copy-start.3 = (s32[16]{0:T(128)S(1)}, s32[16]{0:T(128)}, u32[]{:S(2)}) copy-start(s32[16]{0:T(128)} %offset_ref.1) | copy-start | bytes 196
  83.9 59.3 %copy-start = (f32[4,1,2,256,256]{4,3,2,1,0:T(8,128)S(1)}, f32[4,1,2,256,256]{4,3,2,1,0:T(8,128)}, u32[]{:S(2)}) copy-start(f32[4,1,2,256,256]{4,3,2,1,0:T(8,128)} %param.7) | copy-start | bytes 6291460

commit v3 on v2

v3 whole, which is shorter than its diff:
```python
import jax
import jax.numpy as jnp
from jax import lax
from jax.experimental import pallas as pl
from jax.experimental.pallas import tpu as pltpu
from jax.sharding import Mesh
from jax.sharding import PartitionSpec as P

MIX_RATE = 0.6
PHONON = 0.1
BROADENING = 0.02
GOLDEN = 0.5 + 0.5 * 5.0**0.5

M = 256
PTS = 4
E_TOT = 128
KN = 8
DEVS = 256
ROWS = 16
ORDER = ("xl", "xh", "y", "z", "c")
F32 = jnp.float32
BF16 = jnp.bfloat16


def vmem():
    return pl.BlockSpec(memory_space=pltpu.VMEM)


def smem():
    return pl.BlockSpec(memory_space=pltpu.SMEM)


def split(x):
    high = x.astype(BF16)
    return high, (x - high.astype(F32)).astype(BF16)


def dot3(a, b):
    left = jnp.concatenate([a[0], a[0], a[1]], axis=1)
    right = jnp.concatenate([b[0], b[1], b[0]], axis=0)
    return jnp.dot(left, right, preferred_element_type=F32)


def exchange_rows(x, y, group):
    axis = x.ndim - 2
    even = lax.broadcasted_iota(jnp.int32, x.shape, axis) // group % 2 == 0
    first = jnp.where(even, x, pltpu.roll(y, group, axis))
    second = jnp.where(even, pltpu.roll(x, 8 - group, axis), y)
    return first, second


def transpose_rows(tiles):
    a, c = exchange_rows(tiles[0], tiles[2], 4)
    b, d = exchange_rows(tiles[1], tiles[3], 4)
    return exchange_rows(a, b, 2) + exchange_rows(c, d, 2)


def invert_all(residuals, scales, slow):
    rows = lax.broadcasted_iota(jnp.int32, (M, M), 0)
    cols = lax.broadcasted_iota(jnp.int32, (M, M), 1)
    eye = (rows == cols).astype(F32)
    pairs = [split(r) for r in residuals]
    seconds = [dot3(p, p) for p in pairs]
    thirds = [dot3(split(q), p) for q, p in zip(seconds, pairs)]
    sums = [r + q + t for r, q, t in zip(residuals, seconds, thirds)]
    cubes = [split(t) for t in thirds]
    sixths = [dot3(c, c) + eye for c in cubes]
    quartics = [
        dot3(split(u + GOLDEN * t), split(u - (1.0 / GOLDEN) * t)) for u, t in zip(sixths, thirds)
    ]
    longs = [dot3(split(r), split(q)) for r, q in zip(sums, quartics)]
    return [
        (eye + jnp.where(f, x, r)) * s for f, x, r, s in zip(slow, longs, sums, scales)
    ]


def to_pieces(green, out_ref, base, block):
    slab = slice(block * 64, block * 64 + 64)
    for q, tiles in enumerate(transpose_rows([g[slab].reshape(8, 8, M) for g in green])):
        for t in range(8):
            for half in range(2):
                piece = base + block * 32 + 4 * t + 2 * (q // 2) + half
                rows = slice(q % 2 * 8, q % 2 * 8 + 8)
                out_ref[piece, rows] = tiles[t, :, half * 128 : half * 128 + 128]


def solve_kernel(
    sigma_hbm,
    ham_hbm,
    coup_hbm,
    energy_ref,
    count_ref,
    out_hbm,
    out_ref,
    sigma_ref,
    ham_ref,
    coup_ref,
    sems,
):
    upper, lower = pl.ds(0, M), pl.ds(M, M)
    copies = [
        pltpu.make_async_copy(coup_hbm, coup_ref, sems.at[0]),
        pltpu.make_async_copy(ham_hbm.at[upper], ham_ref.at[upper], sems.at[1]),
        *(
            pltpu.make_async_copy(sigma_hbm.at[p, upper], sigma_ref.at[p, upper], sems.at[2 + p])
            for p in range(PTS)
        ),
        pltpu.make_async_copy(ham_hbm.at[lower], ham_ref.at[lower], sems.at[6]),
        pltpu.make_async_copy(sigma_hbm.at[:, lower], sigma_ref.at[:, lower], sems.at[7]),
    ]
    for copy in copies:
        copy.start()
    rank = (lax.axis_index("xl") * 8 + lax.axis_index("z")) * 2 + lax.axis_index("c")
    points = range(PTS)
    energy = [energy_ref[rank * PTS + p] for p in points]
    slow = [count_ref[rank * PTS + p] > 2 for p in points]
    scale = [1.0 / jnp.full((M, M), e, F32) for e in energy]
    copies[0].wait()
    coupling = split(coup_ref[...])
    turned = split(coup_ref[...].T)
    copies[1].wait()
    residual = []
    for p in points:
        copies[2 + p].wait()
        residual.append((ham_ref[:M] + sigma_ref[p, :M]) * scale[p])
    left = invert_all(residual, scale, slow)
    for copy in copies[6:]:
        copy.wait()
    inverse = [split(x) for x in left]
    coupled = [split(dot3(x, coupling)) for x in inverse]
    back = [split(dot3(turned, x)) for x in inverse]
    residual = [
        (ham_ref[M:] + sigma_ref[p, M:] + dot3(turned, coupled[p])) * scale[p] for p in points
    ]
    right = invert_all(residual, scale, slow)
    through = [split(dot3(c, split(r))) for c, r in zip(coupled, right)]
    sent = []
    for base, green in ((128, right), (0, None)):
        if green is None:
            green = [x + dot3(t, b) for x, t, b in zip(left, through, back)]
        for block in range(4):
            to_pieces(green, out_ref, base, block)
            part = pl.ds(base + 32 * block, 32)
            sem = sems.at[8 + base // 32 + block]
            sent.append(pltpu.make_async_copy(out_ref.at[part], out_hbm.at[part], sem))
            sent[-1].start()
    for copy in sent:
        copy.wait()


def solve(sigma, ham, coupling, energies, counts):
    hbm = pl.BlockSpec(memory_space=pltpu.HBM)
    return pl.pallas_call(
        solve_kernel,
        out_shape=jax.ShapeDtypeStruct((DEVS, ROWS, 128), F32),
        in_specs=[hbm, hbm, hbm, smem(), smem()],
        out_specs=hbm,
        scratch_shapes=[
            pltpu.VMEM((DEVS, ROWS, 128), F32),
            pltpu.VMEM((PTS, 2 * M, M), F32),
            pltpu.VMEM((2 * M, M), F32),
            pltpu.VMEM((M, M), F32),
            pltpu.SemaphoreType.DMA((16,)),
        ],
        compiler_params=pltpu.CompilerParams(vmem_limit_bytes=60 * 1024 * 1024),
        cost_estimate=pl.CostEstimate(flops=6_800_000_000, bytes_accessed=5_000_000, transcendentals=0),
        name="solve_points",
    )(sigma, ham, coupling, energies, counts)


def lorentz(offset):
    scaled = offset / BROADENING
    return 1.0 / (1.0 + scaled * scaled)


def energy_operator(energies):
    columns = jnp.broadcast_to(energies, (E_TOT, E_TOT))
    spacing = columns.T - columns
    values = lorentz(spacing - PHONON) + lorentz(spacing + PHONON)
    values = values / jnp.sum(values, axis=1, keepdims=True)
    wide = E_TOT * 2
    spread = (
        lax.broadcasted_iota(jnp.int32, (wide, E_TOT), 0) // 2
        == lax.broadcasted_iota(jnp.int32, (wide, E_TOT), 1)
    ).astype(BF16)
    gather = (
        lax.broadcasted_iota(jnp.int32, (E_TOT, wide), 1) // 2
        == lax.broadcasted_iota(jnp.int32, (E_TOT, wide), 0)
    ).astype(BF16)
    row_id = lax.broadcasted_iota(jnp.int32, (wide, wide), 0)
    col_id = lax.broadcasted_iota(jnp.int32, (wide, wide), 1)
    same = ((row_id ^ col_id) & 1) == 0
    parts = []
    for part in split(values):
        tall = jnp.dot(spread, part, preferred_element_type=F32).astype(BF16)
        full = jnp.dot(tall, gather, preferred_element_type=F32)
        parts.append(jnp.where(same, full, 0.0).astype(BF16))
    return parts


def mix_momenta(given, weight):
    half = KN // 2
    total = [0.5 * (weight[s] + weight[s + half]) for s in range(half)]
    change = [0.5 * (weight[s] - weight[s + half]) for s in range(half)]
    added = [given[k] + given[k + half] for k in range(half)]
    taken = [given[k] - given[k + half] for k in range(half)]
    first, second = [], []
    for k in range(half):
        cyclic = total[0] * added[k]
        signed = change[0] * taken[k]
        for s in range(1, half):
            cyclic = cyclic + total[s] * added[(k - s) % half]
            term = change[s] * taken[(k - s) % half]
            signed = signed + term if k >= s else signed - term
        first.append(cyclic + signed)
        second.append(cyclic - signed)
    return first + second


def mix_kernel(energy_ref, strength_ref, offset_ref, in_ref, out_ref, x_high, x_low):
    weight = []
    for d in range(KN):
        total = jnp.float32(0.0)
        for j in range(16):
            total = total + jnp.where(offset_ref[j] == d, strength_ref[j], 0.0)
        weight.append(total)
    high, low = energy_operator(energy_ref[...])
    left = jnp.concatenate([high, high, low], axis=1)
    for upper in range(2):
        for device in range(16):
            given = [in_ref[(upper * KN + k) * 16 + device] for k in range(KN)]
            rows = slice((upper * 16 + device) * 8, (upper * 16 + device) * 8 + 8)
            for k, mixed in enumerate(mix_momenta(given, weight)):
                for tile, part in enumerate(split(mixed)):
                    ref = (x_high, x_low)[tile]
                    ref[rows, k * 256 : k * 256 + 128] = part[:8]
                    ref[rows, k * 256 + 128 : k * 256 + 256] = part[8:]
    for k in range(KN):
        lanes = slice(k * 256, k * 256 + 256)
        right = jnp.concatenate([x_high[:, lanes], x_low[:, lanes], x_high[:, lanes]], axis=0)
        mixed = jnp.dot(left, right, preferred_element_type=F32).reshape(32, 8, 256)
        for upper in range(2):
            part = mixed[upper * 16 : upper * 16 + 16]
            first = (upper * KN + k) * 16
            out_ref[first : first + 16, :8] = part[:, :, :128]
            out_ref[first : first + 16, 8:] = part[:, :, 128:]


def mix(energies, strengths, offsets, x):
    return pl.pallas_call(
        mix_kernel,
        out_shape=jax.ShapeDtypeStruct((DEVS, ROWS, 128), F32),
        in_specs=[vmem(), smem(), smem(), vmem()],
        out_specs=vmem(),
        scratch_shapes=[
            pltpu.VMEM((256, 2048), BF16),
            pltpu.VMEM((256, 2048), BF16),
        ],
        compiler_params=pltpu.CompilerParams(vmem_limit_bytes=32 * 1024 * 1024),
        cost_estimate=pl.CostEstimate(flops=900_000_000, bytes_accessed=4_200_000, transcendentals=0),
        name="mix_energies",
    )(energies, strengths, offsets, x)


def blend_kernel(sigma_ref, in_ref, out_hbm, out_ref, sems):
    copies = []
    for block in range(4):
        for t in range(16 * block, 16 * block + 16):
            rows = slice(8 * t, 8 * t + 8)
            for half in range(2):
                lanes = slice(half * 128, half * 128 + 128)
                even = in_ref[4 * t + half]
                odd = in_ref[4 * t + 2 + half]
                tiles = transpose_rows((even[:8], even[8:], odd[:8], odd[8:]))
                for p, tile in enumerate(tiles):
                    old = sigma_ref[p, rows, lanes]
                    out_ref[p, rows, lanes] = (1.0 - MIX_RATE) * old + MIX_RATE * tile
        rows = pl.ds(128 * block, 128)
        copies.append(
            pltpu.make_async_copy(out_ref.at[:, rows], out_hbm.at[:, rows], sems.at[block])
        )
        copies[-1].start()
    for copy in copies:
        copy.wait()


def blend(sigma, x):
    return pl.pallas_call(
        blend_kernel,
        out_shape=jax.ShapeDtypeStruct((PTS, 2 * M, M), F32),
        in_specs=[vmem(), vmem()],
        out_specs=pl.BlockSpec(memory_space=pltpu.HBM),
        scratch_shapes=[pltpu.VMEM((PTS, 2 * M, M), F32), pltpu.SemaphoreType.DMA((4,))],
        compiler_params=pltpu.CompilerParams(vmem_limit_bytes=24 * 1024 * 1024),
        cost_estimate=pl.CostEstimate(flops=2_000_000, bytes_accessed=6_000_000, transcendentals=0),
        name="blend_old",
    )(sigma, x)


def exchange(x):
    return lax.all_to_all(x, ORDER, split_axis=0, concat_axis=0, tiled=True)


def body(sigma_in, hamiltonian, coupling, energies, counts, strengths, offsets):
    sigma = sigma_in.reshape(PTS, 2 * M, M)
    green = solve(sigma, hamiltonian.reshape(2 * M, M), coupling.reshape(M, M), energies, counts)
    columns = exchange(green)
    mixed = mix(energies.reshape(1, E_TOT), strengths, offsets, columns)
    result = exchange(mixed)
    return blend(sigma, result).reshape(sigma_in.shape)


def solution(mesh):
    fine = Mesh(mesh.devices.reshape(2, 8, 2, 2, 4), ("xl", "z", "c", "xh", "y"))
    energy, mom = ("xl", "z", "c"), ("xh", "y")
    return jax.shard_map(
        body,
        mesh=fine,
        in_specs=(
            P(energy, mom, None, None, None),
            P(mom, None, None, None),
            P(mom, None, None),
            P(),
            P(),
            P(),
            P(),
        ),
        out_specs=P(energy, mom, None, None, None),
        check_vma=False,
    )
```

time: 145 us -> 143 us (0.986)
  Pallas kernels: 16.3 us -> 14.1 us
    pallas_call x1, Pallas kernels: 4.16 us -> 2.51 us  [mix(): pl.pallas_call(mix_kernel, out_shape=jax.ShapeDtypeStruct((DEVS, ROWS, 12...]
where the time goes in v3:
time: 143 us; the launch traced here: 142 us
  blocking collectives  128 us (90%)
  Pallas kernels  14.1 us (10%)
    all_to_all x2, blocking collectives, exchange(): return lax.all_to_all(x, ORDER, split_axis=0, concat_axis=0, tiled=True)  128 us
    pallas_call x1, Pallas kernels, solve(): pl.pallas_call(solve_kernel, out_shape=jax.ShapeDtypeStruct((DEVS, ROWS,...  10.1 us

profile of v3, /device:TPU:1, one launch (start us, length us, event | category | flops | bytes accessed | tf_op | source)
XLA Modules:
  0.0 142.5 jit_solution(13915926881865500813)
XLA Ops:
  0.0 10.1 %solve_points.1 = f32[256,16,128]{2,1,0:T(8,128)} custom-call(f32[4,512,256]{2,1,0:T(8,128)} %bitcast.7, f32[512,256]{1,0:T(8,128)} %bitcast.10, f32[256,256]{1,0:T(8,128)} %bitcast.11, f32[128]{0:T(128)} %energy_ref.1, s32[128]{0:T(128)} %count_ref.1), custom_call_target="tpu_custom_call" | custom-call | flops 6800000000 | bytes 5000000 | tf_op jit(solution)/shard_map/solve_points/pallas_call | solution.py:153
  10.1 0.0 copy-start.1
  10.1 0.0 copy-start.2
  10.1 0.0 copy-start.3
  10.1 69.0 %all_to_all.10.in_ref = f32[256,16,128]{2,1,0:T(8,128)S(1)} all-to-all(f32[256,16,128]{2,1,0:T(8,128)} %solve_points.1), channel_id=1, replica_groups=mesh['xl'=2,'z'=8,'c'=2,'xh'=2,'y'=4] {'xl','xh','y','z','c'}, dimensions={0} | all-to-all | bytes 4194304 | tf_op jit(solution)/shard_map/all_to_all | solution.py:301
  79.2 0.0 copy-done.1
  79.2 0.0 copy-done.2
  79.2 0.0 copy-done.3
  79.2 2.5 %mix_energies.1 = f32[256,16,128]{2,1,0:T(8,128)S(1)} custom-call(f32[1,128]{1,0:T(1,128)S(1)} %bitcast.9, f32[16]{0:T(128)S(1)} %copy-done.2, s32[16]{0:T(128)S(1)} %copy-done.3, f32[256,16,128]{2,1,0:T(8,128)S(1)} %all_to_all.10.in_ref), custom_call_target="tpu_custom_call" | custom-call | flops 900000000 | bytes 4200000 | tf_op jit(solution)/shard_map/mix_energies/pallas_call | solution.py:250
  81.7 0.0 copy-start
  81.7 59.3 %all_to_all.11.in_ref = f32[256,16,128]{2,1,0:T(8,128)S(1)} all-to-all(f32[256,16,128]{2,1,0:T(8,128)S(1)} %mix_energies.1), channel_id=1, replica_groups=mesh['xl'=2,'z'=8,'c'=2,'xh'=2,'y'=4] {'xl','xh','y','z','c'}, dimensions={0} | all-to-all | bytes 4194304 | tf_op jit(solution)/shard_map/all_to_all | solution.py:301
  141.0 0.0 copy-done
  141.0 1.5 %blend_old.1 = f32[4,512,256]{2,1,0:T(8,128)} custom-call(f32[4,512,256]{2,1,0:T(8,128)S(1)} %bitcast.8, f32[256,16,128]{2,1,0:T(8,128)S(1)} %all_to_all.11.in_ref), custom_call_target="tpu_custom_call" | custom-call | flops 2000000 | bytes 6000000 | tf_op jit(solution)/shard_map/blend_old/pallas_call | solution.py:288
Async XLA Ops:
  10.1 69.1 %copy-start.1 = (f32[128]{0:T(128)S(1)}, f32[128]{0:T(128)}, u32[]{:S(2)}) copy-start(f32[128]{0:T(128)} %energy_ref.1) | copy-start | bytes 1540
  10.1 69.1 %copy-start.2 = (f32[16]{0:T(128)S(1)}, f32[16]{0:T(128)}, u32[]{:S(2)}) copy-start(f32[16]{0:T(128)} %strength_ref.1) | copy-start | bytes 196
  10.1 69.1 %copy-start.3 = (s32[16]{0:T(128)S(1)}, s32[16]{0:T(128)}, u32[]{:S(2)}) copy-start(s32[16]{0:T(128)} %offset_ref.1) | copy-start | bytes 196
  81.7 59.3 %copy-start = (f32[4,1,2,256,256]{4,3,2,1,0:T(8,128)S(1)}, f32[4,1,2,256,256]{4,3,2,1,0:T(8,128)}, u32[]{:S(2)}) copy-start(f32[4,1,2,256,256]{4,3,2,1,0:T(8,128)} %param.7) | copy-start | bytes 6291460

commit v4 on v3

--- a/solution.py
+++ b/solution.py
@@ -88,13 +88,14 @@
     sigma_hbm,
     ham_hbm,
     coup_hbm,
-    energy_ref,
-    count_ref,
-    out_hbm,
+    energy_hbm,
+    count_hbm,
     out_ref,
     sigma_ref,
     ham_ref,
     coup_ref,
+    energy_ref,
+    count_ref,
     sems,
 ):
     upper, lower = pl.ds(0, M), pl.ds(M, M)
@@ -108,16 +109,24 @@
         pltpu.make_async_copy(ham_hbm.at[lower], ham_ref.at[lower], sems.at[6]),
         pltpu.make_async_copy(sigma_hbm.at[:, lower], sigma_ref.at[:, lower], sems.at[7]),
     ]
+    scalars = [
+        pltpu.make_async_copy(energy_hbm, energy_ref, sems.at[16]),
+        pltpu.make_async_copy(count_hbm, count_ref, sems.at[17]),
+    ]
+    for copy in scalars:
+        copy.start()
     for copy in copies:
         copy.start()
+    copies[0].wait()
+    coupling = split(coup_ref[...])
+    turned = split(coup_ref[...].T)
+    for copy in scalars:
+        copy.wait()
     rank = (lax.axis_index("xl") * 8 + lax.axis_index("z")) * 2 + lax.axis_index("c")
     points = range(PTS)
     energy = [energy_ref[rank * PTS + p] for p in points]
     slow = [count_ref[rank * PTS + p] > 2 for p in points]
-    scale = [1.0 / jnp.full((M, M), e, F32) for e in energy]
-    copies[0].wait()
-    coupling = split(coup_ref[...])
-    turned = split(coup_ref[...].T)
+    scale = [1.0 / jnp.full((1, 1), e, F32) for e in energy]
     copies[1].wait()
     residual = []
     for p in points:
@@ -134,35 +143,32 @@
     ]
     right = invert_all(residual, scale, slow)
     through = [split(dot3(c, split(r))) for c, r in zip(coupled, right)]
-    sent = []
     for base, green in ((128, right), (0, None)):
         if green is None:
             green = [x + dot3(t, b) for x, t, b in zip(left, through, back)]
         for block in range(4):
             to_pieces(green, out_ref, base, block)
-            part = pl.ds(base + 32 * block, 32)
-            sem = sems.at[8 + base // 32 + block]
-            sent.append(pltpu.make_async_copy(out_ref.at[part], out_hbm.at[part], sem))
-            sent[-1].start()
-    for copy in sent:
-        copy.wait()
 
 
 def solve(sigma, ham, coupling, energies, counts):
     hbm = pl.BlockSpec(memory_space=pltpu.HBM)
+    sigma, ham, coupling, energies, counts = (
+        pltpu.with_memory_space_constraint(v, pltpu.HBM) for v in (sigma, ham, coupling, energies, counts)
+    )
     return pl.pallas_call(
         solve_kernel,
         out_shape=jax.ShapeDtypeStruct((DEVS, ROWS, 128), F32),
-        in_specs=[hbm, hbm, hbm, smem(), smem()],
-        out_specs=hbm,
+        in_specs=[hbm] * 5,
+        out_specs=vmem(),
         scratch_shapes=[
-            pltpu.VMEM((DEVS, ROWS, 128), F32),
             pltpu.VMEM((PTS, 2 * M, M), F32),
             pltpu.VMEM((2 * M, M), F32),
             pltpu.VMEM((M, M), F32),
-            pltpu.SemaphoreType.DMA((16,)),
+            pltpu.SMEM((E_TOT,), F32),
+            pltpu.SMEM((E_TOT,), jnp.int32),
+            pltpu.SemaphoreType.DMA((18,)),
         ],
-        compiler_params=pltpu.CompilerParams(vmem_limit_bytes=60 * 1024 * 1024),
+        compiler_params=pltpu.CompilerParams(vmem_limit_bytes=40 * 1024 * 1024),
         cost_estimate=pl.CostEstimate(flops=6_800_000_000, bytes_accessed=5_000_000, transcendentals=0),
         name="solve_points",
     )(sigma, ham, coupling, energies, counts)

time: 143 us -> 141 us (0.986)
  Pallas kernels: 14.1 us -> 12.6 us
    pallas_call x1, Pallas kernels: 10.1 us -> 8.59 us  [solve(): pl.pallas_call(solve_kernel, out_shape=jax.ShapeDtypeStruct((DEVS, ROWS,...]
where the time goes in v4:
time: 141 us
  blocking collectives  128 us (91%)
  Pallas kernels  12.6 us (9%)
    all_to_all x2, blocking collectives, exchange(): return lax.all_to_all(x, ORDER, split_axis=0, concat_axis=0, tiled=True)  128 us
    pallas_call x1, Pallas kernels, solve(): pl.pallas_call(solve_kernel, out_shape=jax.ShapeDtypeStruct((DEVS, ROWS,...  8.59 us

profile of v4, /device:TPU:1, one launch (start us, length us, event | category | flops | bytes accessed | tf_op | source)
XLA Modules:
  0.0 140.7 jit_solution(16297533677746292620)
XLA Ops:
  0.0 8.6 %solve_points.1 = f32[256,16,128]{2,1,0:T(8,128)S(1)} custom-call(f32[4,512,256]{2,1,0:T(8,128)} %bitcast.7, f32[512,256]{1,0:T(8,128)} %bitcast.10, f32[256,256]{1,0:T(8,128)} %bitcast.11, f32[128]{0:T(128)} %energy_hbm.1, s32[128]{0:T(128)} %count_hbm.1), custom_call_target="tpu_custom_call" | custom-call | flops 6800000000 | bytes 5000000 | tf_op jit(solution)/shard_map/solve_points/pallas_call | solution.py:158
  8.6 0.0 copy-start.1
  8.6 0.0 copy-start.2
  8.6 0.0 copy-start.3
  8.6 68.8 %all_to_all.10.in_ref = f32[256,16,128]{2,1,0:T(8,128)S(1)} all-to-all(f32[256,16,128]{2,1,0:T(8,128)S(1)} %solve_points.1), channel_id=1, replica_groups=mesh['xl'=2,'z'=8,'c'=2,'xh'=2,'y'=4] {'xl','xh','y','z','c'}, dimensions={0} | all-to-all | bytes 4194304 | tf_op jit(solution)/shard_map/all_to_all | solution.py:307
  77.5 0.0 copy-done.1
  77.5 0.0 copy-done.2
  77.5 0.0 copy-done.3
  77.5 2.5 %mix_energies.1 = f32[256,16,128]{2,1,0:T(8,128)S(1)} custom-call(f32[1,128]{1,0:T(1,128)S(1)} %bitcast.9, f32[16]{0:T(128)S(1)} %copy-done.2, s32[16]{0:T(128)S(1)} %copy-done.3, f32[256,16,128]{2,1,0:T(8,128)S(1)} %all_to_all.10.in_ref), custom_call_target="tpu_custom_call" | custom-call | flops 900000000 | bytes 4200000 | tf_op jit(solution)/shard_map/mix_energies/pallas_call | solution.py:256
  80.0 0.0 copy-start
  80.0 59.3 %all_to_all.11.in_ref = f32[256,16,128]{2,1,0:T(8,128)S(1)} all-to-all(f32[256,16,128]{2,1,0:T(8,128)S(1)} %mix_energies.1), channel_id=1, replica_groups=mesh['xl'=2,'z'=8,'c'=2,'xh'=2,'y'=4] {'xl','xh','y','z','c'}, dimensions={0} | all-to-all | bytes 4194304 | tf_op jit(solution)/shard_map/all_to_all | solution.py:307
  139.3 0.0 copy-done
  139.3 1.5 %blend_old.1 = f32[4,512,256]{2,1,0:T(8,128)} custom-call(f32[4,512,256]{2,1,0:T(8,128)S(1)} %bitcast.8, f32[256,16,128]{2,1,0:T(8,128)S(1)} %all_to_all.11.in_ref), custom_call_target="tpu_custom_call" | custom-call | flops 2000000 | bytes 6000000 | tf_op jit(solution)/shard_map/blend_old/pallas_call | solution.py:294
Async XLA Ops:
  8.6 68.9 %copy-start.1 = (f32[128]{0:T(128)S(1)}, f32[128]{0:T(128)}, u32[]{:S(2)}) copy-start(f32[128]{0:T(128)} %energy_hbm.1) | copy-start | bytes 1540
  8.6 68.8 %copy-start.2 = (f32[16]{0:T(128)S(1)}, f32[16]{0:T(128)}, u32[]{:S(2)}) copy-start(f32[16]{0:T(128)} %strength_ref.1) | copy-start | bytes 196
  8.6 68.8 %copy-start.3 = (s32[16]{0:T(128)S(1)}, s32[16]{0:T(128)}, u32[]{:S(2)}) copy-start(s32[16]{0:T(128)} %offset_ref.1) | copy-start | bytes 196
  80.0 59.3 %copy-start = (f32[4,1,2,256,256]{4,3,2,1,0:T(8,128)S(1)}, f32[4,1,2,256,256]{4,3,2,1,0:T(8,128)}, u32[]{:S(2)}) copy-start(f32[4,1,2,256,256]{4,3,2,1,0:T(8,128)} %param.7) | copy-start | bytes 6291460

commit v5 on v4

--- a/solution.py
+++ b/solution.py
@@ -24,10 +24,6 @@
 
 def vmem():
     return pl.BlockSpec(memory_space=pltpu.VMEM)
-
-
-def smem():
-    return pl.BlockSpec(memory_space=pltpu.SMEM)
 
 
 def split(x):
@@ -206,8 +202,7 @@
 
 def mix_momenta(given, weight):
     half = KN // 2
-    total = [0.5 * (weight[s] + weight[s + half]) for s in range(half)]
-    change = [0.5 * (weight[s] - weight[s + half]) for s in range(half)]
+    total, change = weight
     added = [given[k] + given[k + half] for k in range(half)]
     taken = [given[k] - given[k + half] for k in range(half)]
     first, second = [], []
@@ -226,17 +221,20 @@
 def mix_kernel(energy_ref, strength_ref, offset_ref, in_ref, out_ref, x_high, x_low):
     weight = []
     for d in range(KN):
-        total = jnp.float32(0.0)
-        for j in range(16):
-            total = total + jnp.where(offset_ref[j] == d, strength_ref[j], 0.0)
-        weight.append(total)
+        chosen = jnp.where(offset_ref[...] == d, strength_ref[...], 0.0)
+        weight.append(jnp.sum(chosen, axis=1, keepdims=True))
+    half = KN // 2
+    halves = [
+        [jnp.broadcast_to(0.5 * (weight[s] + sign * weight[s + half]), (ROWS, 128)) for s in range(half)]
+        for sign in (1.0, -1.0)
+    ]
     high, low = energy_operator(energy_ref[...])
     left = jnp.concatenate([high, high, low], axis=1)
     for upper in range(2):
         for device in range(16):
             given = [in_ref[(upper * KN + k) * 16 + device] for k in range(KN)]
             rows = slice((upper * 16 + device) * 8, (upper * 16 + device) * 8 + 8)
-            for k, mixed in enumerate(mix_momenta(given, weight)):
+            for k, mixed in enumerate(mix_momenta(given, halves)):
                 for tile, part in enumerate(split(mixed)):
                     ref = (x_high, x_low)[tile]
                     ref[rows, k * 256 : k * 256 + 128] = part[:8]
@@ -256,7 +254,7 @@
     return pl.pallas_call(
         mix_kernel,
         out_shape=jax.ShapeDtypeStruct((DEVS, ROWS, 128), F32),
-        in_specs=[vmem(), smem(), smem(), vmem()],
+        in_specs=[vmem()] * 4,
         out_specs=vmem(),
         scratch_shapes=[
             pltpu.VMEM((256, 2048), BF16),
@@ -311,7 +309,7 @@
     sigma = sigma_in.reshape(PTS, 2 * M, M)
     green = solve(sigma, hamiltonian.reshape(2 * M, M), coupling.reshape(M, M), energies, counts)
     columns = exchange(green)
-    mixed = mix(energies.reshape(1, E_TOT), strengths, offsets, columns)
+    mixed = mix(energies.reshape(1, -1), strengths.reshape(1, -1), offsets.reshape(1, -1), columns)
     result = exchange(mixed)
     return blend(sigma, result).reshape(sigma_in.shape)
 

time: 141 us -> 140 us (level)
  no operation moved by 1% of the time
where the time goes in v5:
time: 140 us
  blocking collectives  128 us (91%)
  Pallas kernels  11.9 us (8%)
    all_to_all x2, blocking collectives, exchange(): return lax.all_to_all(x, ORDER, split_axis=0, concat_axis=0, tiled=True)  128 us
    pallas_call x1, Pallas kernels, solve(): pl.pallas_call(solve_kernel, out_shape=jax.ShapeDtypeStruct((DEVS, ROWS,...  8.59 us

profile of v5, /device:TPU:1, one launch (start us, length us, event | category | flops | bytes accessed | tf_op | source)
XLA Modules:
  0.0 140.1 jit_solution(10193692631618084237)
XLA Ops:
  0.0 8.6 %solve_points.1 = f32[256,16,128]{2,1,0:T(8,128)S(1)} custom-call(f32[4,512,256]{2,1,0:T(8,128)} %bitcast.9, f32[512,256]{1,0:T(8,128)} %bitcast.14, f32[256,256]{1,0:T(8,128)} %bitcast.15, f32[128]{0:T(128)} %energy_hbm.1, s32[128]{0:T(128)} %count_hbm.1), custom_call_target="tpu_custom_call" | custom-call | flops 6800000000 | bytes 5000000 | tf_op jit(solution)/shard_map/solve_points/pallas_call | solution.py:154
  8.6 0.0 copy-start.1
  8.6 0.0 copy-start.2
  8.6 0.0 copy-start.3
  8.6 68.8 %all_to_all.10.in_ref = f32[256,16,128]{2,1,0:T(8,128)S(1)} all-to-all(f32[256,16,128]{2,1,0:T(8,128)S(1)} %solve_points.1), channel_id=1, replica_groups=mesh['xl'=2,'z'=8,'c'=2,'xh'=2,'y'=4] {'xl','xh','y','z','c'}, dimensions={0} | all-to-all | bytes 4194304 | tf_op jit(solution)/shard_map/all_to_all | solution.py:305
  77.5 0.0 copy-done.1
  77.5 0.0 copy-done.2
  77.5 0.0 copy-done.3
  77.5 1.9 %mix_energies.1 = f32[256,16,128]{2,1,0:T(8,128)S(1)} custom-call(f32[1,128]{1,0:T(1,128)S(1)} %bitcast.11, f32[1,16]{1,0:T(1,128)S(1)} %bitcast.12, s32[1,16]{1,0:T(1,128)S(1)} %bitcast.13, f32[256,16,128]{2,1,0:T(8,128)S(1)} %all_to_all.10.in_ref), custom_call_target="tpu_custom_call" | custom-call | flops 900000000 | bytes 4200000 | tf_op jit(solution)/shard_map/mix_energies/pallas_call | solution.py:254
  79.3 0.0 copy-start
  79.4 59.3 %all_to_all.11.in_ref = f32[256,16,128]{2,1,0:T(8,128)S(1)} all-to-all(f32[256,16,128]{2,1,0:T(8,128)S(1)} %mix_energies.1), channel_id=1, replica_groups=mesh['xl'=2,'z'=8,'c'=2,'xh'=2,'y'=4] {'xl','xh','y','z','c'}, dimensions={0} | all-to-all | bytes 4194304 | tf_op jit(solution)/shard_map/all_to_all | solution.py:305
  138.6 0.0 copy-done
  138.6 1.5 %blend_old.1 = f32[4,512,256]{2,1,0:T(8,128)} custom-call(f32[4,512,256]{2,1,0:T(8,128)S(1)} %bitcast.10, f32[256,16,128]{2,1,0:T(8,128)S(1)} %all_to_all.11.in_ref), custom_call_target="tpu_custom_call" | custom-call | flops 2000000 | bytes 6000000 | tf_op jit(solution)/shard_map/blend_old/pallas_call | solution.py:292
Async XLA Ops:
  8.6 68.9 %copy-start.1 = (f32[128]{0:T(128)S(1)}, f32[128]{0:T(128)}, u32[]{:S(2)}) copy-start(f32[128]{0:T(128)} %energy_hbm.1) | copy-start | bytes 1540
  8.6 68.8 %copy-start.2 = (f32[16]{0:T(128)S(1)}, f32[16]{0:T(128)}, u32[]{:S(2)}) copy-start(f32[16]{0:T(128)} %param.12) | copy-start | bytes 196
  8.6 68.8 %copy-start.3 = (s32[16]{0:T(128)S(1)}, s32[16]{0:T(128)}, u32[]{:S(2)}) copy-start(s32[16]{0:T(128)} %param.13) | copy-start | bytes 196
  79.3 59.3 %copy-start = (f32[4,1,2,256,256]{4,3,2,1,0:T(8,128)S(1)}, f32[4,1,2,256,256]{4,3,2,1,0:T(8,128)}, u32[]{:S(2)}) copy-start(f32[4,1,2,256,256]{4,3,2,1,0:T(8,128)} %param.7) | copy-start | bytes 6291460

commit v6 on v5

--- a/solution.py
+++ b/solution.py
@@ -15,9 +15,9 @@
 PTS = 4
 E_TOT = 128
 KN = 8
-DEVS = 256
-ROWS = 16
-ORDER = ("xl", "xh", "y", "z", "c")
+CHIPS = 128
+ROWS = 32
+ORDER = ("xl", "xh", "y", "z")
 F32 = jnp.float32
 BF16 = jnp.bfloat16
 
@@ -75,9 +75,8 @@
     for q, tiles in enumerate(transpose_rows([g[slab].reshape(8, 8, M) for g in green])):
         for t in range(8):
             for half in range(2):
-                piece = base + block * 32 + 4 * t + 2 * (q // 2) + half
-                rows = slice(q % 2 * 8, q % 2 * 8 + 8)
-                out_ref[piece, rows] = tiles[t, :, half * 128 : half * 128 + 128]
+                piece = base + block * 16 + 2 * t + half
+                out_ref[piece, q * 8 : q * 8 + 8] = tiles[t, :, half * 128 : half * 128 + 128]
 
 
 def solve_kernel(
@@ -139,7 +138,7 @@
     ]
     right = invert_all(residual, scale, slow)
     through = [split(dot3(c, split(r))) for c, r in zip(coupled, right)]
-    for base, green in ((128, right), (0, None)):
+    for base, green in ((64, right), (0, None)):
         if green is None:
             green = [x + dot3(t, b) for x, t, b in zip(left, through, back)]
         for block in range(4):
@@ -153,7 +152,7 @@
     )
     return pl.pallas_call(
         solve_kernel,
-        out_shape=jax.ShapeDtypeStruct((DEVS, ROWS, 128), F32),
+        out_shape=jax.ShapeDtypeStruct((CHIPS, ROWS, 128), F32),
         in_specs=[hbm] * 5,
         out_specs=vmem(),
         scratch_shapes=[
@@ -175,22 +174,22 @@
     return 1.0 / (1.0 + scaled * scaled)
 
 
-def energy_operator(energies):
+def energy_operator(energies, core):
     columns = jnp.broadcast_to(energies, (E_TOT, E_TOT))
     spacing = columns.T - columns
     values = lorentz(spacing - PHONON) + lorentz(spacing + PHONON)
     values = values / jnp.sum(values, axis=1, keepdims=True)
-    wide = E_TOT * 2
-    spread = (
-        lax.broadcasted_iota(jnp.int32, (wide, E_TOT), 0) // 2
-        == lax.broadcasted_iota(jnp.int32, (wide, E_TOT), 1)
-    ).astype(BF16)
-    gather = (
-        lax.broadcasted_iota(jnp.int32, (E_TOT, wide), 1) // 2
-        == lax.broadcasted_iota(jnp.int32, (E_TOT, wide), 0)
-    ).astype(BF16)
-    row_id = lax.broadcasted_iota(jnp.int32, (wide, wide), 0)
-    col_id = lax.broadcasted_iota(jnp.int32, (wide, wide), 1)
+    wide = E_TOT
+    row_id = lax.broadcasted_iota(jnp.int32, (2 * wide, E_TOT), 0)
+    row_core = jnp.where(row_id < wide, core, 1 - core)
+    local = row_id & (wide - 1)
+    wanted = (local // 8) * 8 + row_core * 4 + (local & 7) // 2
+    spread = (lax.broadcasted_iota(jnp.int32, (2 * wide, E_TOT), 1) == wanted).astype(BF16)
+    col_id = lax.broadcasted_iota(jnp.int32, (E_TOT, wide), 1)
+    wanted = (col_id // 8) * 8 + core * 4 + (col_id & 7) // 2
+    gather = (lax.broadcasted_iota(jnp.int32, (E_TOT, wide), 0) == wanted).astype(BF16)
+    row_id = lax.broadcasted_iota(jnp.int32, (2 * wide, wide), 0)
+    col_id = lax.broadcasted_iota(jnp.int32, (2 * wide, wide), 1)
     same = ((row_id ^ col_id) & 1) == 0
     parts = []
     for part in split(values):
@@ -218,7 +217,9 @@
     return first + second
 
 
-def mix_kernel(energy_ref, strength_ref, offset_ref, in_ref, out_ref, x_high, x_low):
+def mix_kernel(
+    energy_ref, strength_ref, offset_ref, in_ref, own_ref, first_ref, second_ref, x_high, x_low
+):
     weight = []
     for d in range(KN):
         chosen = jnp.where(offset_ref[...] == d, strength_ref[...], 0.0)
@@ -228,42 +229,71 @@
         [jnp.broadcast_to(0.5 * (weight[s] + sign * weight[s + half]), (ROWS, 128)) for s in range(half)]
         for sign in (1.0, -1.0)
     ]
-    high, low = energy_operator(energy_ref[...])
+    high, low = energy_operator(energy_ref[...], lax.axis_index("c"))
     left = jnp.concatenate([high, high, low], axis=1)
     for upper in range(2):
-        for device in range(16):
-            given = [in_ref[(upper * KN + k) * 16 + device] for k in range(KN)]
-            rows = slice((upper * 16 + device) * 8, (upper * 16 + device) * 8 + 8)
+        for z in range(8):
+            given = [in_ref[(upper * KN + k) * 8 + z] for k in range(KN)]
+            rows = slice((upper * 8 + z) * 8, (upper * 8 + z) * 8 + 8)
             for k, mixed in enumerate(mix_momenta(given, halves)):
-                for tile, part in enumerate(split(mixed)):
-                    ref = (x_high, x_low)[tile]
-                    ref[rows, k * 256 : k * 256 + 128] = part[:8]
-                    ref[rows, k * 256 + 128 : k * 256 + 256] = part[8:]
+                for ref, part in zip((x_high, x_low), split(mixed)):
+                    for q in range(4):
+                        lanes = slice((4 * k + q) * 128, (4 * k + q) * 128 + 128)
+                        ref[rows, lanes] = part[8 * q : 8 * q + 8]
     for k in range(KN):
-        lanes = slice(k * 256, k * 256 + 256)
-        right = jnp.concatenate([x_high[:, lanes], x_low[:, lanes], x_high[:, lanes]], axis=0)
-        mixed = jnp.dot(left, right, preferred_element_type=F32).reshape(32, 8, 256)
-        for upper in range(2):
-            part = mixed[upper * 16 : upper * 16 + 16]
-            first = (upper * KN + k) * 16
-            out_ref[first : first + 16, :8] = part[:, :, :128]
-            out_ref[first : first + 16, 8:] = part[:, :, 128:]
+        for pair, other_ref in enumerate((first_ref, second_ref)):
+            lanes = slice((2 * k + pair) * 256, (2 * k + pair) * 256 + 256)
+            right = jnp.concatenate([x_high[:, lanes], x_low[:, lanes], x_high[:, lanes]], axis=0)
+            mixed = jnp.dot(left, right, preferred_element_type=F32).reshape(32, 8, 256)
+            for upper in range(2):
+                own = mixed[upper * 8 : upper * 8 + 8]
+                other = mixed[16 + upper * 8 : 24 + upper * 8]
+                pieces = slice((upper * KN + k) * 8, (upper * KN + k) * 8 + 8)
+                for q in range(2):
+                    columns = slice(q * 128, q * 128 + 128)
+                    row = 16 * pair + 8 * q
+                    own_ref[pieces, row : row + 8] = own[:, :, columns]
+                    other_ref[pieces, 8 * q : 8 * q + 8] = other[:, :, columns]
 
 
 def mix(energies, strengths, offsets, x):
     return pl.pallas_call(
         mix_kernel,
-        out_shape=jax.ShapeDtypeStruct((DEVS, ROWS, 128), F32),
+        out_shape=[
+            jax.ShapeDtypeStruct((CHIPS, ROWS, 128), F32),
+            jax.ShapeDtypeStruct((CHIPS, ROWS // 2, 128), F32),
+            jax.ShapeDtypeStruct((CHIPS, ROWS // 2, 128), F32),
+        ],
         in_specs=[vmem()] * 4,
-        out_specs=vmem(),
-        scratch_shapes=[
-            pltpu.VMEM((256, 2048), BF16),
-            pltpu.VMEM((256, 2048), BF16),
-        ],
+        out_specs=[vmem()] * 3,
+        scratch_shapes=[pltpu.VMEM((128, 4096), BF16), pltpu.VMEM((128, 4096), BF16)],
         compiler_params=pltpu.CompilerParams(vmem_limit_bytes=32 * 1024 * 1024),
-        cost_estimate=pl.CostEstimate(flops=900_000_000, bytes_accessed=4_200_000, transcendentals=0),
+        cost_estimate=pl.CostEstimate(flops=900_000_000, bytes_accessed=6_200_000, transcendentals=0),
         name="mix_energies",
     )(energies, strengths, offsets, x)
+
+
+def add_kernel(own_ref, first_ref, second_ref, out_ref):
+    out_ref[:, : ROWS // 2] = own_ref[:, : ROWS // 2] + first_ref[...]
+    out_ref[:, ROWS // 2 :] = own_ref[:, ROWS // 2 :] + second_ref[...]
+
+
+def add_halves(own, first, second):
+    return pl.pallas_call(
+        add_kernel,
+        out_shape=jax.ShapeDtypeStruct((CHIPS, ROWS, 128), F32),
+        in_specs=[vmem()] * 3,
+        out_specs=vmem(),
+        compiler_params=pltpu.CompilerParams(vmem_limit_bytes=32 * 1024 * 1024),
+        cost_estimate=pl.CostEstimate(flops=600_000, bytes_accessed=6_200_000, transcendentals=0),
+        name="add_halves",
+    )(own, first, second)
+
+
+def mix_in_chip(energies, strengths, offsets, x):
+    own, first, second = mix(energies, strengths, offsets, x)
+    swap = [(0, 1), (1, 0)]
+    return add_halves(own, lax.ppermute(first, "c", swap), lax.ppermute(second, "c", swap))
 
 
 def blend_kernel(sigma_ref, in_ref, out_hbm, out_ref, sems):
@@ -273,9 +303,8 @@
             rows = slice(8 * t, 8 * t + 8)
             for half in range(2):
                 lanes = slice(half * 128, half * 128 + 128)
-                even = in_ref[4 * t + half]
-                odd = in_ref[4 * t + 2 + half]
-                tiles = transpose_rows((even[:8], even[8:], odd[:8], odd[8:]))
+                piece = in_ref[2 * t + half]
+                tiles = transpose_rows([piece[8 * q : 8 * q + 8] for q in range(4)])
                 for p, tile in enumerate(tiles):
                     old = sigma_ref[p, rows, lanes]
                     out_ref[p, rows, lanes] = (1.0 - MIX_RATE) * old + MIX_RATE * tile
@@ -309,7 +338,9 @@
     sigma = sigma_in.reshape(PTS, 2 * M, M)
     green = solve(sigma, hamiltonian.reshape(2 * M, M), coupling.reshape(M, M), energies, counts)
     columns = exchange(green)
-    mixed = mix(energies.reshape(1, -1), strengths.reshape(1, -1), offsets.reshape(1, -1), columns)
+    mixed = mix_in_chip(
+        energies.reshape(1, -1), strengths.reshape(1, -1), offsets.reshape(1, -1), columns
+    )
     result = exchange(mixed)
     return blend(sigma, result).reshape(sigma_in.shape)
 

time: 140 us -> 147 us (1.050)
  waiting for transfers between devices: 0 us -> 3.5 us
  starting transfers between devices: 0 us -> 3.01 us
    ppermute x0 -> x2, waiting for transfers between devices: none -> 3.5 us  [the longest x1 2.01 us: mix_in_chip(): lax.ppermute(first, 'c', swap)]
    ppermute x0 -> x2, starting transfers between devices: none -> 3.01 us  [the longest x1 2.73 us: mix_in_chip(): lax.ppermute(first, 'c', swap)]
    pallas_call x2 -> x3, Pallas kernels: 10.5 us -> 10.9 us  [the longest x1 8.59 us: solve(): pl.pallas_call(solve_kernel, out_shape=jax.ShapeDtypeStruct((CHIPS, ROWS,...]
  transfers between devices with their start and end apart: 0 -> 2, of which waited for: 0 -> 2; matrix products, arithmetic and copies ran while one was open for 0% -> 0% of each run, Pallas kernels for 0% -> 0%
where the time goes in v6:
time: 147 us
  blocking collectives  128 us (87%)
  Pallas kernels  12.4 us (8%)
  waiting for transfers between devices  3.5 us (2%)
  starting transfers between devices  3.01 us (2%)
    all_to_all x2, blocking collectives, exchange(): return lax.all_to_all(x, ORDER, split_axis=0, concat_axis=0, tiled=True)  128 us
    pallas_call x1, Pallas kernels, solve(): pl.pallas_call(solve_kernel, out_shape=jax.ShapeDtypeStruct((CHIPS, ROWS,...  8.59 us
  transfers between devices with their start and end apart: 2, of which 2 were waited for; matrix products, arithmetic and copies ran while one was open for 0% of the time, Pallas kernels for 0%

profile of v6, /device:TPU:1, one launch (start us, length us, event | category | flops | bytes accessed | tf_op | source)
XLA Modules:
  0.0 146.9 jit_solution(13838791588821249505)
XLA Ops:
  0.0 8.6 %solve_points.1 = f32[128,32,128]{2,1,0:T(8,128)S(1)} custom-call(f32[4,512,256]{2,1,0:T(8,128)} %bitcast.9, f32[512,256]{1,0:T(8,128)} %bitcast.14, f32[256,256]{1,0:T(8,128)} %bitcast.15, f32[128]{0:T(128)} %energy_hbm.1, s32[128]{0:T(128)} %count_hbm.1), custom_call_target="tpu_custom_call" | custom-call | flops 6800000000 | bytes 5000000 | tf_op jit(solution)/shard_map/solve_points/pallas_call | solution.py:153
  8.6 0.0 copy-start.1
  8.6 0.0 copy-start.2
  8.6 0.0 copy-start.3
  8.6 69.0 %all_to_all.10.in_ref = f32[128,32,128]{2,1,0:T(8,128)S(1)} all-to-all(f32[128,32,128]{2,1,0:T(8,128)S(1)} %solve_points.1), channel_id=1, replica_groups=mesh['xl'=2,'z'=8,'c'=2,'xh'=2,'y'=4] {'xl','xh','y','z'}, dimensions={0} | all-to-all | bytes 4194304 | tf_op jit(solution)/shard_map/all_to_all | solution.py:334
  77.6 0.0 copy-done.1
  77.6 0.0 copy-done.2
  77.6 0.0 copy-done.3
  77.6 2.0 %mix_energies.1 = (f32[128,32,128]{2,1,0:T(8,128)S(1)}, f32[128,16,128]{2,1,0:T(8,128)S(1)}, f32[128,16,128]{2,1,0:T(8,128)S(1)}) custom-call(f32[1,128]{1,0:T(1,128)S(1)} %bitcast.11, f32[1,16]{1,0:T(1,128)S(1)} %bitcast.12, s32[1,16]{1,0:T(1,128)S(1)} %bitcast.13, f32[128,32,128]{2,1,0:T(8,128)S(1)} %all_to_all.10.in_ref), custom_call_target="tpu_custom_call" | custom-call | flops 900000000 | bytes 6200000 | tf_op jit(solution)/shard_map/mix_energies/pallas_call | solution.py:260
  79.7 2.7 %collective-permute-start = (f32[128,16,128]{2,1,0:T(8,128)S(1)}, f32[128,16,128]{2,1,0:T(8,128)S(1)}, u32[]{:S(2)}, u32[]{:S(2)}) collective-permute-start(f32[128,16,128]{2,1,0:T(8,128)S(1)} %get-tuple-element.9), channel_id=1, source_target_pairs={{0,8},{8,0},{1,9},{9,1},{2,10},{10,2},{3,11},{11,3},{4,12},{12,4},... | collective-permute-start | bytes 3145736 | tf_op jit(solution)/shard_map/ppermute | solution.py:296
  82.4 0.3 collective-permute-start.1
  82.7 2.0 %collective-permute-done.first_ref = f32[128,16,128]{2,1,0:T(8,128)S(1)} collective-permute-done((f32[128,16,128]{2,1,0:T(8,128)S(1)}, f32[128,16,128]{2,1,0:T(8,128)S(1)}, u32[]{:S(2)}, u32[]{:S(2)}) %collective-permute-start) | collective-permute-done | bytes 1048608 | tf_op jit(solution)/shard_map/ppermute | solution.py:296
  84.7 1.5 %collective-permute-done.1.second_ref = f32[128,16,128]{2,1,0:T(8,128)S(1)} collective-permute-done((f32[128,16,128]{2,1,0:T(8,128)S(1)}, f32[128,16,128]{2,1,0:T(8,128)S(1)}, u32[]{:S(2)}, u32[]{:S(2)}) %collective-permute-start.1) | collective-permute-done | bytes 1048608 | tf_op jit(solution)/shard_map/ppermute | solution.py:296
  86.2 0.3 add_halves.1
  86.4 0.0 copy-start
  86.5 58.8 %all_to_all.11.in_ref = f32[128,32,128]{2,1,0:T(8,128)S(1)} all-to-all(f32[128,32,128]{2,1,0:T(8,128)S(1)} %add_halves.1), channel_id=1, replica_groups=mesh['xl'=2,'z'=8,'c'=2,'xh'=2,'y'=4] {'xl','xh','y','z'}, dimensions={0} | all-to-all | bytes 4194304 | tf_op jit(solution)/shard_map/all_to_all | solution.py:334
  145.2 0.0 copy-done
  145.2 1.5 %blend_old.1 = f32[4,512,256]{2,1,0:T(8,128)} custom-call(f32[4,512,256]{2,1,0:T(8,128)S(1)} %bitcast.10, f32[128,32,128]{2,1,0:T(8,128)S(1)} %all_to_all.11.in_ref), custom_call_target="tpu_custom_call" | custom-call | flops 2000000 | bytes 6000000 | tf_op jit(solution)/shard_map/blend_old/pallas_call | solution.py:321
Async XLA Ops:
  8.6 69.0 %copy-start.1 = (f32[128]{0:T(128)S(1)}, f32[128]{0:T(128)}, u32[]{:S(2)}) copy-start(f32[128]{0:T(128)} %energy_hbm.1) | copy-start | bytes 1540
  8.6 69.0 %copy-start.2 = (f32[16]{0:T(128)S(1)}, f32[16]{0:T(128)}, u32[]{:S(2)}) copy-start(f32[16]{0:T(128)} %param.12) | copy-start | bytes 196
  8.6 69.0 %copy-start.3 = (s32[16]{0:T(128)S(1)}, s32[16]{0:T(128)}, u32[]{:S(2)}) copy-start(s32[16]{0:T(128)} %param.13) | copy-start | bytes 196
  79.7 5.0 %collective-permute-start = (f32[128,16,128]{2,1,0:T(8,128)S(1)}, f32[128,16,128]{2,1,0:T(8,128)S(1)}, u32[]{:S(2)}, u32[]{:S(2)}) collective-permute-start(f32[128,16,128]{2,1,0:T(8,128)S(1)} %get-tuple-element.9), channel_id=1, source_target_pairs={{0,8},{8,0},{1,9},{9,1},{2,10},{10,2},{3,11},{11,3},{4,12},{12,4},... | collective-permute-start | bytes 3145736 | tf_op jit(solution)/shard_map/ppermute | solution.py:296
  82.4 3.8 %collective-permute-start.1 = (f32[128,16,128]{2,1,0:T(8,128)S(1)}, f32[128,16,128]{2,1,0:T(8,128)S(1)}, u32[]{:S(2)}, u32[]{:S(2)}) collective-permute-start(f32[128,16,128]{2,1,0:T(8,128)S(1)} %get-tuple-element.10), channel_id=1, source_target_pairs={{0,8},{8,0},{1,9},{9,1},{2,10},{10,2},{3,11},{11,3},{4,12},{12,4},... | collective-permute-start | bytes 3145736 | tf_op jit(solution)/shard_map/ppermute | solution.py:296
  86.4 58.8 %copy-start = (f32[4,1,2,256,256]{4,3,2,1,0:T(8,128)S(1)}, f32[4,1,2,256,256]{4,3,2,1,0:T(8,128)}, u32[]{:S(2)}) copy-start(f32[4,1,2,256,256]{4,3,2,1,0:T(8,128)} %param.7) | copy-start | bytes 6291460

commit v7 on v5

--- a/solution.py
+++ b/solution.py
@@ -111,11 +111,8 @@
     ]
     for copy in scalars:
         copy.start()
-    for copy in copies:
+    for copy in copies[1:6] + copies[:1] + copies[6:]:
         copy.start()
-    copies[0].wait()
-    coupling = split(coup_ref[...])
-    turned = split(coup_ref[...].T)
     for copy in scalars:
         copy.wait()
     rank = (lax.axis_index("xl") * 8 + lax.axis_index("z")) * 2 + lax.axis_index("c")
@@ -131,6 +128,9 @@
     left = invert_all(residual, scale, slow)
     for copy in copies[6:]:
         copy.wait()
+    copies[0].wait()
+    coupling = split(coup_ref[...])
+    turned = split(coup_ref[...].T)
     inverse = [split(x) for x in left]
     coupled = [split(dot3(x, coupling)) for x in inverse]
     back = [split(dot3(turned, x)) for x in inverse]
@@ -200,17 +200,29 @@
     return parts
 
 
+def cyclic_four(a, weight):
+    even, odd, even_change, odd_change = weight
+    sums = a[0] + a[2], a[1] + a[3]
+    gaps = a[0] - a[2], a[1] - a[3]
+    cyclic = even * sums[0] + odd * sums[1], even * sums[1] + odd * sums[0]
+    signed = (
+        even_change * gaps[0] - odd_change * gaps[1],
+        even_change * gaps[1] + odd_change * gaps[0],
+    )
+    return [cyclic[0] + signed[0], cyclic[1] + signed[1], cyclic[0] - signed[0], cyclic[1] - signed[1]]
+
+
 def mix_momenta(given, weight):
     half = KN // 2
     total, change = weight
     added = [given[k] + given[k + half] for k in range(half)]
     taken = [given[k] - given[k + half] for k in range(half)]
     first, second = [], []
+    cycles = cyclic_four(added, total)
     for k in range(half):
-        cyclic = total[0] * added[k]
+        cyclic = cycles[k]
         signed = change[0] * taken[k]
         for s in range(1, half):
-            cyclic = cyclic + total[s] * added[(k - s) % half]
             term = change[s] * taken[(k - s) % half]
             signed = signed + term if k >= s else signed - term
         first.append(cyclic + signed)
@@ -224,10 +236,10 @@
         chosen = jnp.where(offset_ref[...] == d, strength_ref[...], 0.0)
         weight.append(jnp.sum(chosen, axis=1, keepdims=True))
     half = KN // 2
-    halves = [
-        [jnp.broadcast_to(0.5 * (weight[s] + sign * weight[s + half]), (ROWS, 128)) for s in range(half)]
-        for sign in (1.0, -1.0)
-    ]
+    total = [0.5 * (weight[s] + weight[s + half]) for s in range(half)]
+    change = [0.5 * (weight[s] - weight[s + half]) for s in range(half)]
+    total = [0.5 * (total[s] + sign * total[s + 2]) for sign in (1.0, -1.0) for s in range(2)]
+    halves = [[jnp.broadcast_to(w, (ROWS, 128)) for w in part] for part in (total, change)]
     high, low = energy_operator(energy_ref[...])
     left = jnp.concatenate([high, high, low], axis=1)
     for upper in range(2):
@@ -268,8 +280,8 @@
 
 def blend_kernel(sigma_ref, in_ref, out_hbm, out_ref, sems):
     copies = []
-    for block in range(4):
-        for t in range(16 * block, 16 * block + 16):
+    for block in range(8):
+        for t in range(8 * block, 8 * block + 8):
             rows = slice(8 * t, 8 * t + 8)
             for half in range(2):
                 lanes = slice(half * 128, half * 128 + 128)
@@ -279,7 +291,7 @@
                 for p, tile in enumerate(tiles):
                     old = sigma_ref[p, rows, lanes]
                     out_ref[p, rows, lanes] = (1.0 - MIX_RATE) * old + MIX_RATE * tile
-        rows = pl.ds(128 * block, 128)
+        rows = pl.ds(64 * block, 64)
         copies.append(
             pltpu.make_async_copy(out_ref.at[:, rows], out_hbm.at[:, rows], sems.at[block])
         )
@@ -294,7 +306,7 @@
         out_shape=jax.ShapeDtypeStruct((PTS, 2 * M, M), F32),
         in_specs=[vmem(), vmem()],
         out_specs=pl.BlockSpec(memory_space=pltpu.HBM),
-        scratch_shapes=[pltpu.VMEM((PTS, 2 * M, M), F32), pltpu.SemaphoreType.DMA((4,))],
+        scratch_shapes=[pltpu.VMEM((PTS, 2 * M, M), F32), pltpu.SemaphoreType.DMA((8,))],
         compiler_params=pltpu.CompilerParams(vmem_limit_bytes=24 * 1024 * 1024),
         cost_estimate=pl.CostEstimate(flops=2_000_000, bytes_accessed=6_000_000, transcendentals=0),
         name="blend_old",

time: 140 us -> 140 us (level)
  no operation moved by 1% of the time
where the time goes in v7:
time: 140 us
  blocking collectives  128 us (91%)
  Pallas kernels  11.8 us (8%)
    all_to_all x2, blocking collectives, exchange(): return lax.all_to_all(x, ORDER, split_axis=0, concat_axis=0, tiled=True)  128 us
    pallas_call x1, Pallas kernels, solve(): pl.pallas_call(solve_kernel, out_shape=jax.ShapeDtypeStruct((DEVS, ROWS,...  8.52 us

profile of v7, /device:TPU:1, one launch (start us, length us, event | category | flops | bytes accessed | tf_op | source)
XLA Modules:
  0.0 140.0 jit_solution(9223134026946630264)
XLA Ops:
  0.0 8.5 %solve_points.1 = f32[256,16,128]{2,1,0:T(8,128)S(1)} custom-call(f32[4,512,256]{2,1,0:T(8,128)} %bitcast.9, f32[512,256]{1,0:T(8,128)} %bitcast.14, f32[256,256]{1,0:T(8,128)} %bitcast.15, f32[128]{0:T(128)} %energy_hbm.1, s32[128]{0:T(128)} %count_hbm.1), custom_call_target="tpu_custom_call" | custom-call | flops 6800000000 | bytes 5000000 | tf_op jit(solution)/shard_map/solve_points/pallas_call | solution.py:154
  8.5 0.0 copy-start.1
  8.5 0.0 copy-start.2
  8.6 0.0 copy-start.3
  8.6 68.8 %all_to_all.10.in_ref = f32[256,16,128]{2,1,0:T(8,128)S(1)} all-to-all(f32[256,16,128]{2,1,0:T(8,128)S(1)} %solve_points.1), channel_id=1, replica_groups=mesh['xl'=2,'z'=8,'c'=2,'xh'=2,'y'=4] {'xl','xh','y','z','c'}, dimensions={0} | all-to-all | bytes 4194304 | tf_op jit(solution)/shard_map/all_to_all | solution.py:317
  77.4 0.0 copy-done.1
  77.4 0.0 copy-done.2
  77.4 0.0 copy-done.3
  77.4 1.8 %mix_energies.1 = f32[256,16,128]{2,1,0:T(8,128)S(1)} custom-call(f32[1,128]{1,0:T(1,128)S(1)} %bitcast.11, f32[1,16]{1,0:T(1,128)S(1)} %bitcast.12, s32[1,16]{1,0:T(1,128)S(1)} %bitcast.13, f32[256,16,128]{2,1,0:T(8,128)S(1)} %all_to_all.10.in_ref), custom_call_target="tpu_custom_call" | custom-call | flops 900000000 | bytes 4200000 | tf_op jit(solution)/shard_map/mix_energies/pallas_call | solution.py:266
  79.2 0.0 copy-start
  79.2 59.3 %all_to_all.11.in_ref = f32[256,16,128]{2,1,0:T(8,128)S(1)} all-to-all(f32[256,16,128]{2,1,0:T(8,128)S(1)} %mix_energies.1), channel_id=1, replica_groups=mesh['xl'=2,'z'=8,'c'=2,'xh'=2,'y'=4] {'xl','xh','y','z','c'}, dimensions={0} | all-to-all | bytes 4194304 | tf_op jit(solution)/shard_map/all_to_all | solution.py:317
  138.5 0.0 copy-done
  138.5 1.4 %blend_old.1 = f32[4,512,256]{2,1,0:T(8,128)} custom-call(f32[4,512,256]{2,1,0:T(8,128)S(1)} %bitcast.10, f32[256,16,128]{2,1,0:T(8,128)S(1)} %all_to_all.11.in_ref), custom_call_target="tpu_custom_call" | custom-call | flops 2000000 | bytes 6000000 | tf_op jit(solution)/shard_map/blend_old/pallas_call | solution.py:304
Async XLA Ops:
  8.5 68.9 %copy-start.1 = (f32[128]{0:T(128)S(1)}, f32[128]{0:T(128)}, u32[]{:S(2)}) copy-start(f32[128]{0:T(128)} %energy_hbm.1) | copy-start | bytes 1540
  8.5 68.9 %copy-start.2 = (f32[16]{0:T(128)S(1)}, f32[16]{0:T(128)}, u32[]{:S(2)}) copy-start(f32[16]{0:T(128)} %param.12) | copy-start | bytes 196
  8.6 68.8 %copy-start.3 = (s32[16]{0:T(128)S(1)}, s32[16]{0:T(128)}, u32[]{:S(2)}) copy-start(s32[16]{0:T(128)} %param.13) | copy-start | bytes 196
  79.2 59.3 %copy-start = (f32[4,1,2,256,256]{4,3,2,1,0:T(8,128)S(1)}, f32[4,1,2,256,256]{4,3,2,1,0:T(8,128)}, u32[]{:S(2)}) copy-start(f32[4,1,2,256,256]{4,3,2,1,0:T(8,128)} %param.7) | copy-start | bytes 6291460

commit v8 on v7

--- a/solution.py
+++ b/solution.py
@@ -32,9 +32,8 @@
 
 
 def dot3(a, b):
-    left = jnp.concatenate([a[0], a[0], a[1]], axis=1)
-    right = jnp.concatenate([b[0], b[1], b[0]], axis=0)
-    return jnp.dot(left, right, preferred_element_type=F32)
+    stacked = jnp.dot(jnp.concatenate(a, axis=0), b[0], preferred_element_type=F32)
+    return stacked[:M] + (stacked[M:] + jnp.dot(a[0], b[1], preferred_element_type=F32))
 
 
 def exchange_rows(x, y, group):

time: 140 us -> 140 us (level)
  no operation moved by 1% of the time
where the time goes in v8:
time: 140 us
  blocking collectives  128 us (91%)
  Pallas kernels  11.8 us (8%)
    all_to_all x2, blocking collectives, exchange(): return lax.all_to_all(x, ORDER, split_axis=0, concat_axis=0, tiled=True)  128 us
    pallas_call x1, Pallas kernels, solve(): pl.pallas_call(solve_kernel, out_shape=jax.ShapeDtypeStruct((DEVS, ROWS,...  8.54 us

profile of v8, /device:TPU:1, one launch (start us, length us, event | category | flops | bytes accessed | tf_op | source)
XLA Modules:
  0.0 140.0 jit_solution(9786397798229954597)
XLA Ops:
  0.0 8.5 %solve_points.1 = f32[256,16,128]{2,1,0:T(8,128)S(1)} custom-call(f32[4,512,256]{2,1,0:T(8,128)} %bitcast.9, f32[512,256]{1,0:T(8,128)} %bitcast.14, f32[256,256]{1,0:T(8,128)} %bitcast.15, f32[128]{0:T(128)} %energy_hbm.1, s32[128]{0:T(128)} %count_hbm.1), custom_call_target="tpu_custom_call" | custom-call | flops 6800000000 | bytes 5000000 | tf_op jit(solution)/shard_map/solve_points/pallas_call | solution.py:153
  8.5 0.0 copy-start.1
  8.6 0.0 copy-start.2
  8.6 0.0 copy-start.3
  8.6 68.8 %all_to_all.10.in_ref = f32[256,16,128]{2,1,0:T(8,128)S(1)} all-to-all(f32[256,16,128]{2,1,0:T(8,128)S(1)} %solve_points.1), channel_id=1, replica_groups=mesh['xl'=2,'z'=8,'c'=2,'xh'=2,'y'=4] {'xl','xh','y','z','c'}, dimensions={0} | all-to-all | bytes 4194304 | tf_op jit(solution)/shard_map/all_to_all | solution.py:316
  77.4 0.0 copy-done.1
  77.4 0.0 copy-done.2
  77.4 0.0 copy-done.3
  77.4 1.8 %mix_energies.1 = f32[256,16,128]{2,1,0:T(8,128)S(1)} custom-call(f32[1,128]{1,0:T(1,128)S(1)} %bitcast.11, f32[1,16]{1,0:T(1,128)S(1)} %bitcast.12, s32[1,16]{1,0:T(1,128)S(1)} %bitcast.13, f32[256,16,128]{2,1,0:T(8,128)S(1)} %all_to_all.10.in_ref), custom_call_target="tpu_custom_call" | custom-call | flops 900000000 | bytes 4200000 | tf_op jit(solution)/shard_map/mix_energies/pallas_call | solution.py:265
  79.2 0.0 copy-start
  79.2 59.3 %all_to_all.11.in_ref = f32[256,16,128]{2,1,0:T(8,128)S(1)} all-to-all(f32[256,16,128]{2,1,0:T(8,128)S(1)} %mix_energies.1), channel_id=1, replica_groups=mesh['xl'=2,'z'=8,'c'=2,'xh'=2,'y'=4] {'xl','xh','y','z','c'}, dimensions={0} | all-to-all | bytes 4194304 | tf_op jit(solution)/shard_map/all_to_all | solution.py:316
  138.5 0.0 copy-done
  138.5 1.4 %blend_old.1 = f32[4,512,256]{2,1,0:T(8,128)} custom-call(f32[4,512,256]{2,1,0:T(8,128)S(1)} %bitcast.10, f32[256,16,128]{2,1,0:T(8,128)S(1)} %all_to_all.11.in_ref), custom_call_target="tpu_custom_call" | custom-call | flops 2000000 | bytes 6000000 | tf_op jit(solution)/shard_map/blend_old/pallas_call | solution.py:303
Async XLA Ops:
  8.5 68.9 %copy-start.1 = (f32[128]{0:T(128)S(1)}, f32[128]{0:T(128)}, u32[]{:S(2)}) copy-start(f32[128]{0:T(128)} %energy_hbm.1) | copy-start | bytes 1540
  8.6 68.9 %copy-start.2 = (f32[16]{0:T(128)S(1)}, f32[16]{0:T(128)}, u32[]{:S(2)}) copy-start(f32[16]{0:T(128)} %param.12) | copy-start | bytes 196
  8.6 68.8 %copy-start.3 = (s32[16]{0:T(128)S(1)}, s32[16]{0:T(128)}, u32[]{:S(2)}) copy-start(s32[16]{0:T(128)} %param.13) | copy-start | bytes 196
  79.2 59.3 %copy-start = (f32[4,1,2,256,256]{4,3,2,1,0:T(8,128)S(1)}, f32[4,1,2,256,256]{4,3,2,1,0:T(8,128)}, u32[]{:S(2)}) copy-start(f32[4,1,2,256,256]{4,3,2,1,0:T(8,128)} %param.7) | copy-start | bytes 6291460
